TPU v7x, 256 devices: a whole 4x4x8 slice. The times are simulated.
256 devices in a mesh: frame: 16 (over z_hi, y, core), row: 16 (over x, z_lo).
Axes of the slice: x: 4, y: 4, z: 8 (z_hi: 2, z_lo: 4; z = z_hi * 4 + z_lo), core: 2. Of those that a mesh axis runs over, the one named last changes fastest.
Arguments:
- latent: bfloat16 [64, 32, 240, 320], P('frame', 'row'), may hold values from -6 to 6
- gain_one: float32 [320], replicated, may hold values from 0.1 to 1.9
- spatial_weight: bfloat16 [3, 3, 320, 320], replicated, may hold values from -0.109375 to 0.109375
- gain_two: float32 [320], replicated, may hold values from 0.1 to 1.9
- temporal_weight: bfloat16 [3, 320, 320], replicated, may hold values from -0.1875 to 0.1875
- gain_three: float32 [320], replicated, may hold values from 0.1 to 1.9
- query_weight: bfloat16 [320, 320], replicated, as said below
- key_weight: bfloat16 [320, 320], replicated, may hold values from -0.3125 to 0.3125
- value_weight: bfloat16 [320, 320], replicated, may hold values from -0.3125 to 0.3125
- out_weight: bfloat16 [320, 320], replicated, may hold values from -0.3125 to 0.3125
Outputs:
- block_out: float32 [64, 32, 240, 320], P('frame', 'row')
Inputs may be any that keep to these rules, and one draw needn't show every extreme that they name: `query_weight`: a projection matrix.
All inputs are finite; a program needn't handle non-finite values.
Results may differ from a plain program's by a relative error of at most 0.012.
The roundings to bfloat16 on the way count: a program that leaves them out, or rounds other values in their place, can miss the bound.
Values may be sent and summed in bfloat16 or wider, within the bound.
A program may use at most 128 MiB of HBM per device.

v0:
```python
import jax
import jax.numpy as jnp
from jax import lax
from jax.sharding import PartitionSpec as P

HEAD_DIM = 64


def extended(cells, sides, width):
    for axis, dim in sides:
        count = lax.axis_size(axis)
        ends = count - 1
        head = lax.slice_in_dim(cells, 0, width, axis=dim)
        tail = lax.slice_in_dim(cells, cells.shape[dim] - width, cells.shape[dim], axis=dim)
        cells = jnp.concatenate(
            [
                lax.ppermute(tail, axis, [(i, (i + 1) % count) for i in range(ends)]),
                cells,
                lax.ppermute(head, axis, [((i + 1) % count, i) for i in range(ends)]),
            ],
            axis=dim,
        )
    return cells


def rms_norm(values, gain):
    mean_sq = jnp.mean(values * values, axis=-1, keepdims=True)
    return values * lax.rsqrt(mean_sq + 1e-06) * gain


def project(normed, weight):
    chans = normed.shape[-1]
    flat = jnp.dot(normed.reshape(-1, chans), weight, preferred_element_type=jnp.float32)
    return flat.astype(jnp.bfloat16).reshape(normed.shape[:-1] + (weight.shape[1],))


def attend_heads(queries, keys, values):
    frames, pixels, chans = queries.shape
    heads = chans // HEAD_DIM
    q_split = queries.reshape(frames, pixels, heads, HEAD_DIM)
    k_split = keys.reshape(frames, pixels, heads, HEAD_DIM)
    v_split = values.reshape(frames, pixels, heads, HEAD_DIM)
    scores = jnp.einsum(
        "fphd,gphd->phfg", q_split, k_split, preferred_element_type=jnp.float32
    ) / jnp.sqrt(jnp.float32(HEAD_DIM))
    peak = jnp.max(scores, axis=-1, keepdims=True)
    expo = jnp.exp(scores - peak)
    total = jnp.sum(expo, axis=-1)
    weight = expo.astype(jnp.bfloat16)
    summed = jnp.einsum("phfg,gphd->fphd", weight, v_split, preferred_element_type=jnp.float32)
    summed = summed / jnp.transpose(total, (2, 0, 1))[..., None]
    return summed.reshape(frames, pixels, chans).astype(jnp.bfloat16)


def temporal_mix(padded, temporal_weight, frames):
    chans = padded.shape[-1]
    pixels = padded.shape[1]
    total = jnp.zeros((frames * pixels, chans), jnp.float32)
    for tap in range(3):
        total = total + jnp.dot(
            padded[tap : tap + frames].reshape(-1, chans),
            temporal_weight[tap],
            preferred_element_type=jnp.float32,
        )
    return total.reshape(frames, pixels, chans)


def local(
    latent,
    gain_one,
    spatial_weight,
    gain_two,
    temporal_weight,
    gain_three,
    query_weight,
    key_weight,
    value_weight,
    out_weight,
):
    frames_here, rows_here, width, chans = latent.shape
    source = latent.astype(jnp.float32)
    act_one = jax.nn.silu(rms_norm(source, gain_one)).astype(jnp.bfloat16)
    rimmed = extended(act_one, (("row", 1),), 1)
    spatial = lax.conv_general_dilated(
        rimmed,
        spatial_weight,
        (1, 1),
        ((0, 0), (1, 1)),
        dimension_numbers=("NHWC", "HWIO", "NHWC"),
        preferred_element_type=jnp.float32,
    )
    hidden_one = source + spatial
    pixels = rows_here * width
    hidden_flat = hidden_one.reshape(frames_here, pixels, chans)
    act_two = jax.nn.silu(rms_norm(hidden_flat, gain_two)).astype(jnp.bfloat16)
    padded = extended(act_two, (("frame", 0),), 1)
    temporal = temporal_mix(padded, temporal_weight, frames_here)
    hidden_two = hidden_flat + temporal
    normed = rms_norm(hidden_two, gain_three).astype(jnp.bfloat16)
    groups = lax.axis_size("frame")
    per_group = pixels // groups

    def attend_triple(triple):
        shape_in = triple[0].shape
        flat_q = triple[0].reshape(shape_in[0], shape_in[2], chans)
        flat_k = triple[1].reshape(shape_in[0], shape_in[2], chans)
        flat_v = triple[2].reshape(shape_in[0], shape_in[2], chans)
        return attend_heads(flat_q, flat_k, flat_v).reshape(shape_in)

    triple = (
        project(normed, query_weight).reshape(frames_here, groups, per_group, chans),
        project(normed, key_weight).reshape(frames_here, groups, per_group, chans),
        project(normed, value_weight).reshape(frames_here, groups, per_group, chans),
    )
    attended = attend_triple(
        (
            lax.all_to_all(triple[0], "frame", split_axis=1, concat_axis=0, tiled=True),
            lax.all_to_all(triple[1], "frame", split_axis=1, concat_axis=0, tiled=True),
            lax.all_to_all(triple[2], "frame", split_axis=1, concat_axis=0, tiled=True),
        )
    )
    returned = lax.all_to_all(attended, "frame", split_axis=0, concat_axis=1, tiled=True)
    mixed = jnp.dot(returned.reshape(-1, chans), out_weight, preferred_element_type=jnp.float32)
    result = hidden_two.reshape(-1, chans) + mixed
    return result.reshape(frames_here, rows_here, width, chans)


def solution(mesh):
    return jax.shard_map(
        local,
        mesh=mesh,
        in_specs=(P("frame", "row", None, None), P(), P(), P(), P(), P(), P(), P(), P(), P()),
        out_specs=P("frame", "row", None, None),
        check_vma=False,
    )
```

profile of v0, /device:TPU:39, one launch (start us, length us, event | category | flops | bytes accessed | tf_op | source)
XLA Modules:
  0.0 389.2 jit_solution(17123246703365757660)
XLA Ops:
  0.0 2.7 copy.64
  13.0 3.5 collective-permute-start
  16.5 11.6 %collective-permute-done.1 = bf16[4,1,240,320]{2,3,1,0:T(8,128)(2,1)} collective-permute-done((bf16[4,1,240,320]{2,3,1,0:T(8,128)(2,1)}, bf16[4,1,240,320]{2,3,1,0:T(8,128)(2,1)}, u32[]{:S(2)}, u32[]{:S(2)}) %collective-permute-start.1) | collective-permute-done | bytes 614432 | tf_op jit(solution)/shard_map/ppermute | solution.py:19
  29.5 15.3 %collective-permute-done = bf16[4,1,240,320]{2,3,1,0:T(8,128)(2,1)} collective-permute-done((bf16[4,1,240,320]{2,3,1,0:T(8,128)(2,1)}, bf16[4,1,240,320]{2,3,1,0:T(8,128)(2,1)}, u32[]{:S(2)}, u32[]{:S(2)}) %collective-permute-start) | collective-permute-done | bytes 614432 | tf_op jit(solution)/shard_map/ppermute | solution.py:17
  49.2 2.9 pad
  52.1 5.8 %reshape.116 = bf16[4,4,8,31,320]{4,3,2,1,0:T(8,128)(2,1)} reshape(bf16[4,4,248,320]{3,2,1,0:T(8,128)(2,1)} %pad) | data formatting | bytes 5079040 | tf_op jit(solution)/shard_map/conv_general_dilated | solution.py:84
  61.6 6.6 %fusion.24 = f32[2,32,31,320]{3,1,2,0:T(8,128)S(1)} fusion(bf16[3,3,320,320]{3,2,1,0:T(8,128)(2,1)S(1)} %copy-done, bf16[4,4,8,33,320]{4,3,2,1,0:T(8,128)(2,1)S(1)} %fusion.4, pred[32,31]{0,1:T(8,128)(4,1)S(1)} %copy-done.16), kind=kOutput, calls=%fused_computation.43 | convolution fusion | flops 3657543680 | bytes 7087072 | tf_op jit(solution)/shard_map/conv_general_dilated | solution.py:84
  71.7 2.8 multiply_reduce_fusion.2
  74.5 3.3 copy.72
  77.8 3.4 copy.71
  83.1 4.9 %copy.75 = bf16[4,2,240,320]{2,1,0,3:T(2,128)(2,1)} copy(bf16[4,2,240,320]{3,2,0,1:T(8,128)(2,1)} %multiply_convert_fusion) | data formatting | bytes 2457600 | tf_op jit(solution)/shard_map/convert_element_type | solution.py:95
  88.0 5.3 %convert_element_type.48 = bf16[1920,320]{0,1:T(8,128)(2,1)} reshape(bf16[4,2,240,320]{2,1,0,3:T(2,128)(2,1)} %copy.75) | data formatting | bytes 2457600 | tf_op jit(solution)/shard_map/convert_element_type | solution.py:95
  93.3 4.8 %reshape.108 = f32[4,480,320]{1,2,0:T(8,128)} reshape(f32[4,2,240,320]{2,1,3,0:T(2,128)} %copy.72) | data formatting | bytes 4915200 | tf_op jit(solution)/shard_map/reshape | solution.py:94
  98.2 2.6 multiply_convert_fusion.1
  102.9 3.4 collective-permute-start.3
  106.3 3.1 collective-permute-start.2
  109.4 5.1 %reshape.107 = f32[1920,320]{0,1:T(8,128)} reshape(f32[4,2,240,320]{2,1,0,3:T(2,128)} %copy.71) | data formatting | bytes 4915200 | tf_op jit(solution)/shard_map/reshape | solution.py:94
  114.5 3.7 fusion.32
  122.6 3.9 %reshape.109 = bf16[1920,320]{0,1:T(8,128)(2,1)} reshape(bf16[4,480,320]{1,0,2:T(4,128)(2,1)} %copy.74) | data formatting | bytes 2457600 | tf_op jit(solution)/shard_map/reshape | solution.py:61
  126.6 3.4 copy.76
  130.0 4.0 %reshape.110 = bf16[1920,320]{0,1:T(8,128)(2,1)} reshape(bf16[4,480,320]{1,0,2:T(4,128)(2,1)} %copy.76) | data formatting | bytes 2457600 | tf_op jit(solution)/shard_map/reshape | solution.py:61
  134.0 3.2 convolution_add_fusion.2
  137.2 3.3 convolution_add_fusion.1
  140.4 6.7 %reshape.111 = f32[4,2,240,320]{2,1,0,3:T(2,128)} reshape(f32[1920,320]{0,1:T(8,128)} %convolution_add_fusion.1) | data formatting | bytes 4915200 | tf_op jit(solution)/shard_map/reshape | solution.py:65
  147.1 5.7 %copy.77 = f32[4,2,240,320]{3,2,0,1:T(8,128)} copy(f32[4,2,240,320]{2,1,0,3:T(2,128)} %reshape.111) | data formatting | bytes 4915200 | tf_op jit(solution)/shard_map/reshape | solution.py:65
  155.3 4.3 %multiply_convert_fusion.2 = (bf16[1920,320]{0,1:T(8,128)(2,1)S(1)}, f32[1920,320]{0,1:T(8,128)}) fusion(f32[320]{0:T(512)S(1)} %copy-done.15, f32[1920]{0:T(1024)S(1)} %rsqrt.35, f32[1920,320]{0,1:T(8,128)} %reshape.107, f32[1920,320]{0,1:T(8,128)} %convolution_add_fusion.1), kind=kLoop, calls=%fused_computation.42 | loop fusion | flops 2457600 | bytes 8610560 | tf_op jit(solution)/shard_map/convert_element_type | solution.py:99
  162.0 2.5 reshape_reshape.22
  166.8 14.6 %all-to-all-start.2 = ((bf16[4,16,30,320]{3,0,2,1:T(4,128)(2,1)}), bf16[4,16,30,320]{3,0,2,1:T(4,128)(2,1)}, u32[]{:S(2)}, u32[]{:S(2)}) async-start(bf16[4,16,30,320]{3,0,2,1:T(4,128)(2,1)} %copy.86), calls=%async_computation.2 | async-start | bytes 2949120 | tf_op jit(solution)/shard_map/all_to_all | solution.py:118
  183.9 2.5 reshape_reshape.20
  188.7 32.6 %all-to-all-done.2 = bf16[4,16,30,320]{3,0,2,1:T(4,128)(2,1)} async-done(((bf16[4,16,30,320]{3,0,2,1:T(4,128)(2,1)}), bf16[4,16,30,320]{3,0,2,1:T(4,128)(2,1)}, u32[]{:S(2)}, u32[]{:S(2)}) %all-to-all-start.2) | async-done | bytes 1228832 | tf_op jit(solution)/shard_map/all_to_all | solution.py:118
  221.3 5.0 %all-to-all-start.1 = ((bf16[4,16,30,320]{3,0,2,1:T(4,128)(2,1)}), bf16[4,16,30,320]{3,0,2,1:T(4,128)(2,1)S(1)}, u32[]{:S(2)}, u32[]{:S(2)}) async-start(bf16[4,16,30,320]{3,0,2,1:T(4,128)(2,1)} %copy.83), calls=%async_computation.1 | async-start | bytes 2949120 | tf_op jit(solution)/shard_map/all_to_all | solution.py:117
  228.3 2.5 copy.79
  230.8 2.5 reshape_reshape.18
  235.7 27.8 %all-to-all-done.1 = bf16[4,16,30,320]{3,0,2,1:T(4,128)(2,1)S(1)} async-done(((bf16[4,16,30,320]{3,0,2,1:T(4,128)(2,1)}), bf16[4,16,30,320]{3,0,2,1:T(4,128)(2,1)S(1)}, u32[]{:S(2)}, u32[]{:S(2)}) %all-to-all-start.1) | async-done | bytes 1228832 | tf_op jit(solution)/shard_map/all_to_all | solution.py:117
  263.5 5.3 %all-to-all-start = ((bf16[4,16,30,320]{3,0,2,1:T(4,128)(2,1)}), bf16[4,16,30,320]{3,0,2,1:T(4,128)(2,1)S(1)}, u32[]{:S(2)}, u32[]{:S(2)}) async-start(bf16[4,16,30,320]{3,0,2,1:T(4,128)(2,1)} %copy.80), calls=%async_computation | async-start | bytes 2949120 | tf_op jit(solution)/shard_map/all_to_all | solution.py:119
  268.8 3.3 copy.87
  272.1 5.5 %reshape_reshape.23 = bf16[64,30,5,64]{3,2,0,1:T(8,128)(2,1)} reshape(bf16[16,4,1,30,320]{4,1,0,3,2:T(4,128)(2,1)} %copy.87) | data formatting | bytes 2457600 | tf_op jit(solution)/shard_map/reshape;reshape | solution.py:41
  279.6 5.5 %reshape_reshape.21 = bf16[64,30,5,64]{3,2,0,1:T(8,128)(2,1)} reshape(bf16[16,4,1,30,320]{4,1,0,3,2:T(4,128)(2,1)} %copy.84) | data formatting | bytes 2457600 | tf_op jit(solution)/shard_map/reshape;reshape | solution.py:40
  285.1 20.7 %all-to-all-done = bf16[4,16,30,320]{3,0,2,1:T(4,128)(2,1)S(1)} async-done(((bf16[4,16,30,320]{3,0,2,1:T(4,128)(2,1)}), bf16[4,16,30,320]{3,0,2,1:T(4,128)(2,1)S(1)}, u32[]{:S(2)}, u32[]{:S(2)}) %all-to-all-start) | async-done | bytes 1228832 | tf_op jit(solution)/shard_map/all_to_all | solution.py:119
  306.6 3.6 reshape_reshape.19
  310.2 4.7 %multiply_reduce_fusion = (f32[30,5,64]{2,1,0:T(8,128)S(1)}, f32[30,5,64,64]{2,3,1,0:T(8,128)S(1)}) fusion(bf16[64,30,5,64]{3,2,0,1:T(8,128)(2,1)} %reshape_reshape.23, bf16[64,30,5,64]{3,2,0,1:T(8,128)(2,1)} %reshape_reshape.21), kind=kOutput, calls=%fused_computation.5 | convolution fusion | flops 79862400 | bytes 4953600 | tf_op jit(solution)/shard_map/fphd,gphd->phfg/dot_general | solution.py:43
  317.1 2.7 fusion.1
  319.8 3.9 %copy.92 = bf16[64,1,30,320]{3,2,1,0:T(8,128)(2,1)S(1)} copy(bf16[64,1,30,320]{0,3,2,1:T(8,128)(2,1)} %bitcast.80) | data formatting | bytes 2457600 | tf_op jit(solution)/shard_map/convert_element_type | solution.py:52
  323.7 44.2 %all_to_all.60 = bf16[64,1,30,320]{3,2,1,0:T(8,128)(2,1)S(1)} all-to-all(bf16[64,1,30,320]{3,2,1,0:T(8,128)(2,1)S(1)} %copy.92), channel_id=1, replica_groups=mesh['frame'=16,'row'=16] {'frame'}, dimensions={0} | all-to-all | bytes 2457600 | tf_op jit(solution)/shard_map/all_to_all | solution.py:122
  370.7 3.5 reshape.112
  374.3 3.7 convolution_add_fusion
  378.0 6.9 %reshape.113 = f32[4,2,240,320]{2,1,0,3:T(2,128)} reshape(f32[1920,320]{0,1:T(8,128)} %convolution_add_fusion) | data formatting | bytes 4915200 | tf_op jit(solution)/shard_map/reshape | solution.py:125
  384.9 4.1 %copy.95 = f32[4,2,240,320]{2,3,1,0:T(8,128)} copy(f32[4,2,240,320]{2,1,0,3:T(2,128)} %reshape.113) | data formatting | bytes 4915200 | tf_op jit(solution)/shard_map/reshape | solution.py:125
  (74 shorter events, 55.5 us)
Async XLA Ops:
  0.0 61.6 %copy-start = (bf16[3,3,320,320]{3,2,1,0:T(8,128)(2,1)S(1)}, bf16[3,3,320,320]{3,2,1,0:T(8,128)(2,1)}, u32[]{:S(2)}) copy-start(bf16[3,3,320,320]{3,2,1,0:T(8,128)(2,1)} %param.12) | copy-start | bytes 5529604
  0.0 4.6 %copy-start.14 = (f32[320]{0:T(512)S(1)}, f32[320]{0:T(512)}, u32[]{:S(2)}) copy-start(f32[320]{0:T(512)} %param.11) | copy-start | bytes 3844
  2.7 1.9 copy-start.2
  5.5 1.1 copy-start.3
  9.9 18.2 %collective-permute-start.1 = (bf16[4,1,240,320]{2,3,1,0:T(8,128)(2,1)}, bf16[4,1,240,320]{2,3,1,0:T(8,128)(2,1)}, u32[]{:S(2)}, u32[]{:S(2)}) collective-permute-start(bf16[4,1,240,320]{2,3,1,0:T(8,128)(2,1)} %copy.66), channel_id=1, source_target_pairs={{1,0},{2,1},{3,2},{4,3},{5,4},{6,5},{7,6},{8,7},{9,8},{10,9},{11,1... | collective-permute-start | bytes 1843208 | tf_op jit(solution)/shard_map/ppermute | solution.py:19
  13.0 31.9 %collective-permute-start = (bf16[4,1,240,320]{2,3,1,0:T(8,128)(2,1)}, bf16[4,1,240,320]{2,3,1,0:T(8,128)(2,1)}, u32[]{:S(2)}, u32[]{:S(2)}) collective-permute-start(bf16[4,1,240,320]{2,3,1,0:T(8,128)(2,1)} %copy.65), channel_id=1, source_target_pairs={{0,1},{1,2},{2,3},{3,4},{4,5},{5,6},{6,7},{7,8},{8,9},{9,10},{10,1... | collective-permute-start | bytes 1843208 | tf_op jit(solution)/shard_map/ppermute | solution.py:17
  59.2 2.4 copy-start.16
  77.8 3.4 copy-start.13
  100.9 1.1 copy-start.5
  102.9 15.3 %collective-permute-start.3 = (bf16[1,480,320]{1,2,0:T(8,128)(2,1)}, bf16[1,480,320]{1,2,0:T(8,128)(2,1)S(1)}, u32[]{:S(2)}, u32[]{:S(2)}) collective-permute-start(bf16[1,480,320]{1,2,0:T(8,128)(2,1)} %get-tuple-element.13), channel_id=1, source_target_pairs={{16,0},{32,16},{48,32},{64,48},{80,64},{96,80},{112,96},{128,112},... | collective-permute-start | bytes 921608 | tf_op jit(solution)/shard_map/ppermute | solution.py:19
  106.3 11.9 %collective-permute-start.2 = (bf16[1,480,320]{1,2,0:T(8,128)(2,1)}, bf16[1,480,320]{1,2,0:T(8,128)(2,1)}, u32[]{:S(2)}, u32[]{:S(2)}) collective-permute-start(bf16[1,480,320]{1,2,0:T(8,128)(2,1)} %get-tuple-element.14), channel_id=1, source_target_pairs={{0,16},{16,32},{32,48},{48,64},{64,80},{80,96},{96,112},{112,128},... | collective-permute-start | bytes 921608 | tf_op jit(solution)/shard_map/ppermute | solution.py:17
  114.5 3.7 copy-start.6
  134.0 3.2 copy-start.7
  152.8 2.4 copy-start.15
  155.2 4.3 %copy-start.10 = (bf16[320,320]{1,0:T(8,128)(2,1)S(1)}, bf16[320,320]{1,0:T(8,128)(2,1)}, u32[]{:S(2)}) copy-start(bf16[320,320]{1,0:T(8,128)(2,1)} %param.17) | copy-start | bytes 614404
  164.6 16.9 %copy-start.11 = (bf16[320,320]{1,0:T(8,128)(2,1)S(1)}, bf16[320,320]{1,0:T(8,128)(2,1)}, u32[]{:S(2)}) copy-start(bf16[320,320]{1,0:T(8,128)(2,1)} %param.16) | copy-start | bytes 614404
  166.8 54.5 %all-to-all-start.2 = ((bf16[4,16,30,320]{3,0,2,1:T(4,128)(2,1)}), bf16[4,16,30,320]{3,0,2,1:T(4,128)(2,1)}, u32[]{:S(2)}, u32[]{:S(2)}) async-start(bf16[4,16,30,320]{3,0,2,1:T(4,128)(2,1)} %copy.86), calls=%async_computation.2 | async-start | bytes 2949120 | tf_op jit(solution)/shard_map/all_to_all | solution.py:118
  186.4 39.9 %copy-start.12 = (bf16[320,320]{1,0:T(8,128)(2,1)S(1)}, bf16[320,320]{1,0:T(8,128)(2,1)}, u32[]{:S(2)}) copy-start(bf16[320,320]{1,0:T(8,128)(2,1)} %param.18) | copy-start | bytes 614404
  221.3 42.2 %all-to-all-start.1 = ((bf16[4,16,30,320]{3,0,2,1:T(4,128)(2,1)}), bf16[4,16,30,320]{3,0,2,1:T(4,128)(2,1)S(1)}, u32[]{:S(2)}, u32[]{:S(2)}) async-start(bf16[4,16,30,320]{3,0,2,1:T(4,128)(2,1)} %copy.83), calls=%async_computation.1 | async-start | bytes 2949120 | tf_op jit(solution)/shard_map/all_to_all | solution.py:117
  263.5 42.3 %all-to-all-start = ((bf16[4,16,30,320]{3,0,2,1:T(4,128)(2,1)}), bf16[4,16,30,320]{3,0,2,1:T(4,128)(2,1)S(1)}, u32[]{:S(2)}, u32[]{:S(2)}) async-start(bf16[4,16,30,320]{3,0,2,1:T(4,128)(2,1)} %copy.80), calls=%async_computation | async-start | bytes 2949120 | tf_op jit(solution)/shard_map/all_to_all | solution.py:119
  314.9 2.1 copy-start.8
  368.7 5.6 %copy-start.4 = (f32[1920,320]{0,1:T(8,128)S(1)}, f32[1920,320]{0,1:T(8,128)}, u32[]{:S(2)}) copy-start(f32[1920,320]{0,1:T(8,128)} %get-tuple-element.6) | copy-start | bytes 7372804
  368.7 5.6 %copy-start.9 = (bf16[320,320]{1,0:T(8,128)(2,1)S(1)}, bf16[320,320]{1,0:T(8,128)(2,1)}, u32[]{:S(2)}) copy-start(bf16[320,320]{1,0:T(8,128)(2,1)} %param.19) | copy-start | bytes 614404
  378.0 10.9 %copy-start.1 = (bf16[3,3,320,320]{3,2,1,0:T(8,128)(2,1)S(1)}, bf16[3,3,320,320]{3,2,1,0:T(8,128)(2,1)}, u32[]{:S(2)}) copy-start(bf16[3,3,320,320]{3,2,1,0:T(8,128)(2,1)} %param.12) | copy-start | bytes 5529604
where the time goes:
time: 395 us; the launch traced here: 389 us
  local copies, waits for them, and re-layouts  143 us (36%)
  waiting for transfers between devices  108 us (27%)
  blocking collectives  44.2 us (11%)
  starting transfers between devices  36.9 us (9%)
  matrix products  31.5 us (8%)
  other arithmetic  25 us (6%)
    all_to_all x1, blocking collectives, local(): lax.all_to_all(attended, 'frame', split_axis=0, concat_axis=1, tiled=True)  44.2 us
    all_to_all x1, waiting for transfers between devices, local(): lax.all_to_all(triple[1], 'frame', split_axis=1, concat_axis=0, tiled=True)  32.6 us
    all_to_all x1, waiting for transfers between devices, local(): lax.all_to_all(triple[0], 'frame', split_axis=1, concat_axis=0, tiled=True)  27.8 us
    all_to_all x1, waiting for transfers between devices, local(): lax.all_to_all(triple[2], 'frame', split_axis=1, concat_axis=0, tiled=True)  20.7 us
    ppermute x2, waiting for transfers between devices, extended(): lax.ppermute(tail, axis, [(i, (i + 1) % count) for i in range(ends)])  15.3 us
    all_to_all x1, starting transfers between devices, local(): lax.all_to_all(triple[1], 'frame', split_axis=1, concat_axis=0, tiled=True)  14.6 us
    reshape x2, local copies, waits for them, and re-layouts, temporal_mix(): return total.reshape(frames, pixels, chans)  12.4 us
    ppermute x2, waiting for transfers between devices, extended(): lax.ppermute(head, axis, [((i + 1) % count, i) for i in range(ends)])  11.6 us
  transfers between devices with their start and end apart: 7, of which 5 were waited for; matrix products, arithmetic and copies ran while one was open for 11% of the time, Pallas kernels for 0%

commit v1 on v0

--- a/solution.py
+++ b/solution.py
@@ -100,25 +100,13 @@
     groups = lax.axis_size("frame")
     per_group = pixels // groups
 
-    def attend_triple(triple):
-        shape_in = triple[0].shape
-        flat_q = triple[0].reshape(shape_in[0], shape_in[2], chans)
-        flat_k = triple[1].reshape(shape_in[0], shape_in[2], chans)
-        flat_v = triple[2].reshape(shape_in[0], shape_in[2], chans)
-        return attend_heads(flat_q, flat_k, flat_v).reshape(shape_in)
-
-    triple = (
-        project(normed, query_weight).reshape(frames_here, groups, per_group, chans),
-        project(normed, key_weight).reshape(frames_here, groups, per_group, chans),
-        project(normed, value_weight).reshape(frames_here, groups, per_group, chans),
+    moved = lax.all_to_all(
+        normed.reshape(frames_here, groups, per_group, chans), "frame", split_axis=1, concat_axis=0, tiled=True
     )
-    attended = attend_triple(
-        (
-            lax.all_to_all(triple[0], "frame", split_axis=1, concat_axis=0, tiled=True),
-            lax.all_to_all(triple[1], "frame", split_axis=1, concat_axis=0, tiled=True),
-            lax.all_to_all(triple[2], "frame", split_axis=1, concat_axis=0, tiled=True),
-        )
-    )
+    moved = moved.reshape(frames_here * groups, per_group, chans)
+    attended = attend_heads(
+        project(moved, query_weight), project(moved, key_weight), project(moved, value_weight)
+    ).reshape(frames_here * groups, 1, per_group, chans)
     returned = lax.all_to_all(attended, "frame", split_axis=0, concat_axis=1, tiled=True)
     mixed = jnp.dot(returned.reshape(-1, chans), out_weight, preferred_element_type=jnp.float32)
     result = hidden_two.reshape(-1, chans) + mixed

time: 395 us -> 397 us (level)
  the two profiles are of different devices: /device:TPU:39 before, /device:TPU:63 now
where the time goes in v1:
time: 397 us; the launch traced here: 391 us
  local copies, waits for them, and re-layouts  195 us (49%)
  waiting for transfers between devices  62.7 us (16%)
  blocking collectives  48.7 us (12%)
  matrix products  34.7 us (9%)
  other arithmetic  26.2 us (7%)
  starting transfers between devices  23.4 us (6%)
    all_to_all x1, blocking collectives, local(): lax.all_to_all(normed.reshape(frames_here, groups, per_group, chans), 'fr...  48.7 us
    all_to_all x1, waiting for transfers between devices, local(): lax.all_to_all(attended, 'frame', split_axis=0, concat_axis=1, tiled=True)  31.6 us
    another operation x2, local copies, waits for them, and re-layouts, attend_heads(): k_split = keys.reshape(frames, pixels, heads, HEAD_DIM)  25.6 us
    another operation x2, local copies, waits for them, and re-layouts, attend_heads(): q_split = queries.reshape(frames, pixels, heads, HEAD_DIM)  25.3 us
    another operation x2, local copies, waits for them, and re-layouts, attend_heads(): v_split = values.reshape(frames, pixels, heads, HEAD_DIM)  22.7 us
    ppermute x2, waiting for transfers between devices, extended(): lax.ppermute(tail, axis, [(i, (i + 1) % count) for i in range(ends)])  16.5 us
    reshape x3, local copies, waits for them, and re-layouts, temporal_mix(): return total.reshape(frames, pixels, chans)  16.4 us
    ppermute x2, waiting for transfers between devices, extended(): lax.ppermute(head, axis, [((i + 1) % count, i) for i in range(ends)])  14.6 us
  transfers between devices with their start and end apart: 5, of which 5 were waited for; matrix products, arithmetic and copies ran while one was open for 4% of the time, Pallas kernels for 0%

profile of v1, /device:TPU:63, one launch (start us, length us, event | category | flops | bytes accessed | tf_op | source)
XLA Modules:
  0.0 391.0 jit_solution(15593227416273346015)
XLA Ops:
  14.2 3.5 collective-permute-start
  17.7 11.6 %collective-permute-done.1 = bf16[4,1,240,320]{2,3,1,0:T(8,128)(2,1)} collective-permute-done((bf16[4,1,240,320]{2,3,1,0:T(8,128)(2,1)}, bf16[4,1,240,320]{2,3,1,0:T(8,128)(2,1)}, u32[]{:S(2)}, u32[]{:S(2)}) %collective-permute-start.1) | collective-permute-done | bytes 614432 | tf_op jit(solution)/shard_map/ppermute | solution.py:19
  30.8 15.3 %collective-permute-done = bf16[4,1,240,320]{2,3,1,0:T(8,128)(2,1)} collective-permute-done((bf16[4,1,240,320]{2,3,1,0:T(8,128)(2,1)}, bf16[4,1,240,320]{2,3,1,0:T(8,128)(2,1)}, u32[]{:S(2)}, u32[]{:S(2)}) %collective-permute-start) | collective-permute-done | bytes 614432 | tf_op jit(solution)/shard_map/ppermute | solution.py:17
  50.5 2.9 pad
  53.4 5.8 %reshape.119 = bf16[4,4,8,31,320]{4,3,2,1,0:T(8,128)(2,1)} reshape(bf16[4,4,248,320]{3,2,1,0:T(8,128)(2,1)} %pad) | data formatting | bytes 5079040 | tf_op jit(solution)/shard_map/conv_general_dilated | solution.py:84
  62.8 6.6 %fusion.25 = f32[2,32,31,320]{3,1,2,0:T(8,128)S(1)} fusion(bf16[3,3,320,320]{3,2,1,0:T(8,128)(2,1)S(1)} %copy-done, bf16[4,4,8,33,320]{4,3,2,1,0:T(8,128)(2,1)S(1)} %fusion.4, pred[32,31]{0,1:T(8,128)(4,1)S(1)} %copy-done.15), kind=kOutput, calls=%fused_computation.42 | convolution fusion | flops 3657543680 | bytes 7087072 | tf_op jit(solution)/shard_map/conv_general_dilated | solution.py:84
  69.4 3.4 copy.76
  72.8 4.2 %reshape.123 = f32[2,4,248,320]{3,2,1,0:T(8,128)} reshape(f32[2,32,31,320]{3,2,1,0:T(8,128)} %copy.76) | data formatting | bytes 5079040 | tf_op jit(solution)/shard_map/conv_general_dilated | solution.py:84
  77.0 2.8 multiply_reduce_fusion.2
  79.7 3.5 copy.78
  83.2 2.8 copy.83
  88.1 4.9 %copy.81 = bf16[4,2,240,320]{2,1,0,3:T(2,128)(2,1)} copy(bf16[4,2,240,320]{3,2,0,1:T(8,128)(2,1)} %multiply_convert_fusion) | data formatting | bytes 2457600 | tf_op jit(solution)/shard_map/convert_element_type | solution.py:95
  93.0 4.9 %convert_element_type.48 = bf16[1920,320]{0,1:T(8,128)(2,1)} reshape(bf16[4,2,240,320]{2,1,0,3:T(2,128)(2,1)} %copy.81) | data formatting | bytes 2457600 | tf_op jit(solution)/shard_map/convert_element_type | solution.py:95
  97.9 4.8 %reshape.109 = f32[4,480,320]{1,2,0:T(8,128)} reshape(f32[4,2,240,320]{2,1,3,0:T(2,128)} %copy.78) | data formatting | bytes 4915200 | tf_op jit(solution)/shard_map/reshape | solution.py:94
  102.7 2.7 multiply_convert_fusion.1
  105.5 3.4 collective-permute-start.3
  108.9 8.1 %collective-permute-start.2 = (bf16[1,480,320]{1,2,0:T(8,128)(2,1)S(1)}, bf16[1,480,320]{1,2,0:T(8,128)(2,1)S(1)}, u32[]{:S(2)}, u32[]{:S(2)}) collective-permute-start(bf16[1,480,320]{1,2,0:T(8,128)(2,1)S(1)} %get-tuple-element.12), channel_id=1, source_target_pairs={{0,16},{16,32},{32,48},{48,64},{64,80},{80,96},{96,112},{112,128},... | collective-permute-start | bytes 921608 | tf_op jit(solution)/shard_map/ppermute | solution.py:17
  117.1 3.3 fusion.29
  120.3 3.1 collective-permute-done.3
  128.0 4.3 %reshape.111 = bf16[1920,320]{0,1:T(8,128)(2,1)} reshape(bf16[4,480,320]{1,0,2:T(4,128)(2,1)} %copy.82) | data formatting | bytes 2457600 | tf_op jit(solution)/shard_map/reshape | solution.py:61
  132.3 3.4 copy.80
  135.7 4.0 %reshape.110 = bf16[1920,320]{0,1:T(8,128)(2,1)} reshape(bf16[4,480,320]{1,0,2:T(4,128)(2,1)} %copy.80) | data formatting | bytes 2457600 | tf_op jit(solution)/shard_map/reshape | solution.py:61
  139.7 3.2 convolution_add_fusion.2
  142.9 3.3 convolution_add_fusion.1
  146.2 6.7 %reshape.114 = f32[4,2,240,320]{2,1,0,3:T(2,128)} reshape(f32[1920,320]{0,1:T(8,128)} %convolution_add_fusion.1) | data formatting | bytes 4915200 | tf_op jit(solution)/shard_map/reshape | solution.py:65
  152.9 3.4 copy.84
  156.3 5.6 %copy.86 = f32[4,2,240,320]{3,2,0,1:T(8,128)} copy(f32[4,2,240,320]{2,1,0,3:T(2,128)} %reshape.114) | data formatting | bytes 4915200 | tf_op jit(solution)/shard_map/reshape | solution.py:65
  164.4 4.1 %reshape.113 = f32[4,16,30,320]{3,2,1,0:T(8,128)} reshape(f32[1920,320]{1,0:T(8,128)} %copy.84) | data formatting | bytes 4915200 | tf_op jit(solution)/shard_map/reshape | solution.py:65
  168.5 5.0 %fusion.18 = bf16[4,16,30,320]{3,0,2,1:T(4,128)(2,1)S(1)} fusion(f32[4,16,30,320]{3,0,2,1:T(4,128)} %bitcast.76, f32[4,16,30,320]{3,2,1,0:T(8,128)} %reshape.113, f32[320]{0:T(512)S(1)} %copy-done.14, f32[4,16,30]{0,2,1:T(8,128)S(1)} %copy.88), kind=kLoop, calls=%fused_computation.28 | loop fusion | flops 2457600 | bytes 6152960 | tf_op jit(solution)/shard_map/convert_element_type | solution.py:99
  173.5 48.7 %all_to_all.30 = bf16[4,16,30,320]{3,0,2,1:T(4,128)(2,1)S(1)} all-to-all(bf16[4,16,30,320]{3,0,2,1:T(4,128)(2,1)S(1)} %fusion.18), channel_id=1, replica_groups=mesh['frame'=16,'row'=16] {'frame'}, dimensions={1} | all-to-all | bytes 2457600 | tf_op jit(solution)/shard_map/all_to_all | solution.py:103
  223.7 3.6 reshape_reshape.14
  227.3 3.5 convolution_convert_fusion
  234.6 15.4 %reshape.127 = bf16[64,30,5,64]{1,0,3,2:T(8,128)(2,1)} reshape(bf16[1920,320]{0,1:T(8,128)(2,1)} %convolution_convert_fusion.2) | data formatting | bytes 2457600 | tf_op jit(solution)/shard_map/reshape;reshape | solution.py:42
  250.0 7.3 %copy.95 = bf16[64,30,5,64]{0,3,2,1:T(8,128)(2,1)} copy(bf16[64,30,5,64]{1,0,3,2:T(8,128)(2,1)} %reshape.127) | data formatting | bytes 2457600 | tf_op jit(solution)/shard_map/reshape;reshape | solution.py:42
  257.3 15.4 %reshape.128 = bf16[64,30,5,64]{1,0,3,2:T(8,128)(2,1)} reshape(bf16[1920,320]{0,1:T(8,128)(2,1)} %convolution_convert_fusion.1) | data formatting | bytes 2457600 | tf_op jit(solution)/shard_map/reshape;reshape | solution.py:40
  272.7 9.9 %copy.93 = bf16[64,30,5,64]{3,0,2,1:T(8,128)(2,1)} copy(bf16[64,30,5,64]{1,0,3,2:T(8,128)(2,1)} %reshape.128) | data formatting | bytes 2457600 | tf_op jit(solution)/shard_map/reshape;reshape | solution.py:40
  282.6 15.6 %reshape.129 = bf16[64,30,5,64]{1,0,3,2:T(8,128)(2,1)} reshape(bf16[1920,320]{0,1:T(8,128)(2,1)} %convolution_convert_fusion) | data formatting | bytes 2457600 | tf_op jit(solution)/shard_map/reshape;reshape | solution.py:41
  298.2 10.0 %copy.94 = bf16[64,30,5,64]{3,0,2,1:T(8,128)(2,1)} copy(bf16[64,30,5,64]{1,0,3,2:T(8,128)(2,1)} %reshape.129) | data formatting | bytes 2457600 | tf_op jit(solution)/shard_map/reshape;reshape | solution.py:41
  308.2 3.9 multiply_reduce_fusion
  316.5 4.7 %copy.97 = bf16[64,1,30,320]{3,2,1,0:T(8,128)(2,1)} copy(bf16[64,1,30,320]{0,3,2,1:T(8,128)(2,1)} %bitcast.79) | data formatting | bytes 2457600 | tf_op jit(solution)/shard_map/convert_element_type | solution.py:52
  321.2 6.4 %all-to-all-start.1 = ((bf16[64,1,30,320]{3,2,1,0:T(8,128)(2,1)}), bf16[64,1,30,320]{3,2,1,0:T(8,128)(2,1)}, u32[]{:S(2)}, u32[]{:S(2)}) async-start(bf16[64,1,30,320]{3,2,1,0:T(8,128)(2,1)} %copy.97), calls=%async_computation.1 | async-start | bytes 3145728 | tf_op jit(solution)/shard_map/all_to_all | solution.py:110
  327.6 3.3 copy.77
  330.9 5.0 %reshape.108 = f32[1920,320]{0,1:T(8,128)} reshape(f32[4,2,240,320]{2,1,0,3:T(2,128)} %copy.77) | data formatting | bytes 4915200 | tf_op jit(solution)/shard_map/reshape | solution.py:94
  335.9 31.6 %all-to-all-done.1 = bf16[64,1,30,320]{3,2,1,0:T(8,128)(2,1)} async-done(((bf16[64,1,30,320]{3,2,1,0:T(8,128)(2,1)}), bf16[64,1,30,320]{3,2,1,0:T(8,128)(2,1)}, u32[]{:S(2)}, u32[]{:S(2)}) %all-to-all-start.1) | async-done | bytes 1228832 | tf_op jit(solution)/shard_map/all_to_all | solution.py:110
  371.8 3.5 reshape.115
  375.3 4.5 %convolution_add_fusion = f32[1920,320]{0,1:T(8,128)} fusion(bf16[1920,320]{1,0:T(8,128)(2,1)} %reshape.115, bf16[320,320]{1,0:T(8,128)(2,1)S(1)} %copy-done.11, f32[1920,320]{0,1:T(8,128)} %reshape.108, f32[1920,320]{0,1:T(8,128)S(1)} %copy-done.2), kind=kOutput, calls=%fused_computation.32 | convolution fusion | flops 394444800 | bytes 8806400 | tf_op jit(solution)/shard_map/dot_general | solution.py:111
  379.8 6.9 %reshape.116 = f32[4,2,240,320]{2,1,0,3:T(2,128)} reshape(f32[1920,320]{0,1:T(8,128)} %convolution_add_fusion) | data formatting | bytes 4915200 | tf_op jit(solution)/shard_map/reshape | solution.py:113
  386.7 4.1 %copy.100 = f32[4,2,240,320]{2,3,1,0:T(8,128)} copy(f32[4,2,240,320]{2,1,0,3:T(2,128)} %reshape.116) | data formatting | bytes 4915200 | tf_op jit(solution)/shard_map/reshape | solution.py:113
  (65 shorter events, 46.8 us)
Async XLA Ops:
  0.0 62.8 %copy-start = (bf16[3,3,320,320]{3,2,1,0:T(8,128)(2,1)S(1)}, bf16[3,3,320,320]{3,2,1,0:T(8,128)(2,1)}, u32[]{:S(2)}) copy-start(bf16[3,3,320,320]{3,2,1,0:T(8,128)(2,1)} %param.12) | copy-start | bytes 5529604
  0.0 4.5 %copy-start.13 = (f32[320]{0:T(512)S(1)}, f32[320]{0:T(512)}, u32[]{:S(2)}) copy-start(f32[320]{0:T(512)} %param.11) | copy-start | bytes 3844
  6.8 1.1 copy-start.4
  11.2 18.2 %collective-permute-start.1 = (bf16[4,1,240,320]{2,3,1,0:T(8,128)(2,1)}, bf16[4,1,240,320]{2,3,1,0:T(8,128)(2,1)}, u32[]{:S(2)}, u32[]{:S(2)}) collective-permute-start(bf16[4,1,240,320]{2,3,1,0:T(8,128)(2,1)} %copy.72), channel_id=1, source_target_pairs={{1,0},{2,1},{3,2},{4,3},{5,4},{6,5},{7,6},{8,7},{9,8},{10,9},{11,1... | collective-permute-start | bytes 1843208 | tf_op jit(solution)/shard_map/ppermute | solution.py:19
  14.2 31.9 %collective-permute-start = (bf16[4,1,240,320]{2,3,1,0:T(8,128)(2,1)}, bf16[4,1,240,320]{2,3,1,0:T(8,128)(2,1)}, u32[]{:S(2)}, u32[]{:S(2)}) collective-permute-start(bf16[4,1,240,320]{2,3,1,0:T(8,128)(2,1)} %copy.71), channel_id=1, source_target_pairs={{0,1},{1,2},{2,3},{3,4},{4,5},{5,6},{6,7},{7,8},{8,9},{9,10},{10,1... | collective-permute-start | bytes 1843208 | tf_op jit(solution)/shard_map/ppermute | solution.py:17
  60.4 2.4 copy-start.15
  83.2 2.9 copy-start.12
  102.7 14.4 %copy-start.5 = (bf16[1920,320]{0,1:T(8,128)(2,1)S(1)}, bf16[1920,320]{0,1:T(8,128)(2,1)}, u32[]{:S(2)}) copy-start(bf16[1920,320]{0,1:T(8,128)(2,1)} %convert_element_type.48) | copy-start | bytes 3686404
  105.5 17.9 %collective-permute-start.3 = (bf16[1,480,320]{1,2,0:T(8,128)(2,1)S(1)}, bf16[1,480,320]{1,2,0:T(8,128)(2,1)S(1)}, u32[]{:S(2)}, u32[]{:S(2)}) collective-permute-start(bf16[1,480,320]{1,2,0:T(8,128)(2,1)S(1)} %get-tuple-element.11), channel_id=1, source_target_pairs={{16,0},{32,16},{48,32},{64,48},{80,64},{96,80},{112,96},{128,112},... | collective-permute-start | bytes 921608 | tf_op jit(solution)/shard_map/ppermute | solution.py:19
  108.9 15.7 %collective-permute-start.2 = (bf16[1,480,320]{1,2,0:T(8,128)(2,1)S(1)}, bf16[1,480,320]{1,2,0:T(8,128)(2,1)S(1)}, u32[]{:S(2)}, u32[]{:S(2)}) collective-permute-start(bf16[1,480,320]{1,2,0:T(8,128)(2,1)S(1)} %get-tuple-element.12), channel_id=1, source_target_pairs={{0,16},{16,32},{32,48},{48,64},{64,80},{80,96},{96,112},{112,128},... | collective-permute-start | bytes 921608 | tf_op jit(solution)/shard_map/ppermute | solution.py:17
  139.7 3.2 copy-start.6
  164.4 4.1 %copy-start.14 = (f32[320]{0:T(512)S(1)}, f32[320]{0:T(512)}, u32[]{:S(2)}) copy-start(f32[320]{0:T(512)} %param.15) | copy-start | bytes 3844
  222.3 5.0 %copy-start.8 = (bf16[320,320]{1,0:T(8,128)(2,1)S(1)}, bf16[320,320]{1,0:T(8,128)(2,1)}, u32[]{:S(2)}) copy-start(bf16[320,320]{1,0:T(8,128)(2,1)} %param.17) | copy-start | bytes 614404
  223.7 7.0 %copy-start.9 = (bf16[320,320]{1,0:T(8,128)(2,1)S(1)}, bf16[320,320]{1,0:T(8,128)(2,1)}, u32[]{:S(2)}) copy-start(bf16[320,320]{1,0:T(8,128)(2,1)} %param.16) | copy-start | bytes 614404
  227.3 3.5 copy-start.3
  227.3 5.4 %copy-start.10 = (bf16[320,320]{1,0:T(8,128)(2,1)S(1)}, bf16[320,320]{1,0:T(8,128)(2,1)}, u32[]{:S(2)}) copy-start(bf16[320,320]{1,0:T(8,128)(2,1)} %param.18) | copy-start | bytes 614404
  312.1 1.7 copy-start.7
  321.2 46.4 %all-to-all-start.1 = ((bf16[64,1,30,320]{3,2,1,0:T(8,128)(2,1)}), bf16[64,1,30,320]{3,2,1,0:T(8,128)(2,1)}, u32[]{:S(2)}, u32[]{:S(2)}) async-start(bf16[64,1,30,320]{3,2,1,0:T(8,128)(2,1)} %copy.97), calls=%async_computation.1 | async-start | bytes 3145728 | tf_op jit(solution)/shard_map/all_to_all | solution.py:110
  369.7 5.6 %copy-start.2 = (f32[1920,320]{0,1:T(8,128)S(1)}, f32[1920,320]{0,1:T(8,128)}, u32[]{:S(2)}) copy-start(f32[1920,320]{0,1:T(8,128)} %convolution_add_fusion.1) | copy-start | bytes 7372804
  369.7 5.6 %copy-start.11 = (bf16[320,320]{1,0:T(8,128)(2,1)S(1)}, bf16[320,320]{1,0:T(8,128)(2,1)}, u32[]{:S(2)}) copy-start(bf16[320,320]{1,0:T(8,128)(2,1)} %param.19) | copy-start | bytes 614404
  379.8 10.9 %copy-start.1 = (bf16[3,3,320,320]{3,2,1,0:T(8,128)(2,1)S(1)}, bf16[3,3,320,320]{3,2,1,0:T(8,128)(2,1)}, u32[]{:S(2)}) copy-start(bf16[3,3,320,320]{3,2,1,0:T(8,128)(2,1)} %param.12) | copy-start | bytes 5529604

commit v2 on v1

v2 whole, which is shorter than its diff:
```python
import functools

import jax
import jax.numpy as jnp
from jax import lax
from jax.experimental import pallas as pl
from jax.experimental.pallas import tpu as pltpu
from jax.sharding import PartitionSpec as P

MESH = pl.DeviceIdType.MESH
F32 = jnp.float32
BF16 = jnp.bfloat16
C = 320
D = 64
ORDER = (0, 3, 1, 2)


def rms(v, gain):
    mean_sq = jnp.sum(v * v, axis=-1, keepdims=True) * (1.0 / C)
    return v * lax.rsqrt(mean_sq + 1e-06) * gain


def silu(v):
    return v / (1.0 + jnp.exp(-v))


def dot(a, b):
    return jnp.dot(a, b, preferred_element_type=F32)


def main_kernel(
    lat, g1, g2, g3, ws_h, wt_h, wq_h, wk_h, wv_h, wo_h,
    out,
    ws, wt, wq, wk, wv, wo,
    pad, send1, recv1, hid, act, hal, act2, edge, nsend, nrecv,
    qb, kb, vb, ab, asend, arecv, zsend,
    wsem, s1, r1, sx, rx, sf, rf, sn, rn, sa, ra, sz, rz, lsem,
):
    me_f = lax.axis_index("frame")
    me_r = lax.axis_index("row")
    z_hi, j = me_f // 8, me_f % 8
    x, z_lo = me_r // 4, me_r % 4
    z = z_hi * 4 + z_lo

    def dev_z(t):
        return {"frame": (t // 4) * 8 + j, "row": x * 4 + t % 4}

    def dev_x(t):
        return {"frame": me_f, "row": t * 4 + z_lo}

    def dev_j(t):
        return {"frame": z_hi * 8 + t, "row": me_r}

    bar = pltpu.get_barrier_semaphore()
    for k in range(1, 8):
        pl.semaphore_signal(bar, 1, device_id=dev_z((z + k) % 8), device_id_type=MESH)
        pl.semaphore_signal(bar, 1, device_id=dev_j((j + k) % 8), device_id_type=MESH)
    for k in (1, 3):
        pl.semaphore_signal(bar, 1, device_id=dev_x((x + k) % 4), device_id_type=MESH)

    loads = [
        pltpu.make_async_copy(a, b, wsem.at[n])
        for n, (a, b) in enumerate(
            ((ws_h, ws), (wt_h, wt), (wq_h, wq), (wk_h, wk), (wv_h, wv), (wo_h, wo))
        )
    ]
    for cp in loads:
        cp.start()

    def remote(src, dst, ss, rs, dev):
        return pltpu.make_async_remote_copy(src, dst, ss, rs, device_id=dev, device_id_type=MESH)

    def z1(k, i):
        t = (z + k) % 8
        return remote(send1.at[t, i], recv1.at[z, i], s1.at[k, i], r1.at[k, i], dev_z(t))

    pad[0:8] = jnp.zeros((8, 2 * C), F32)
    pad[248:256] = jnp.zeros((8, 2 * C), F32)
    for n, i in enumerate(ORDER):
        pad[8:248, 0:C] = lat[i, 0].astype(F32)
        pad[8:248, C : 2 * C] = lat[i, 1].astype(F32)

        for t in range(8):
            send1[t, i] = pad[7 + 30 * t : 39 + 30 * t, :].astype(BF16)
        if n == 0:
            pl.semaphore_wait(bar, 16)
        for k in range(1, 8):
            z1(k, i).start()
        recv1[z, i] = send1[z, i]

    def hx(s, side):
        t = (x + (3 if side else 1)) % 4
        row = 1 if side else 8
        return remote(
            act.at[s, :, row], hal.at[s, side], sx.at[s, side], rx.at[s, side], dev_x(t)
        )

    def hf(side):
        t = (j + (7 if side else 1)) % 8
        slot = 1 if side else 4
        return remote(act2.at[:, slot], edge.at[side], sf.at[side], rf.at[side], dev_j(t))

    def activate(s, i):
        for k in range(1, 8):
            src = (z + 8 - k) % 8
            remote(send1.at[src, i], recv1.at[src, i], s1.at[k, i], r1.at[k, i], dev_z(src)).wait_recv()

        def one(q, _):
            grp, zl = q // 4, q % 4
            both = recv1[q, i].astype(F32)
            for r in range(2):
                v = both[:, r * C : (r + 1) * C]
                hid[grp * 4 + i, 2 * zl + r] = v
                act[s, grp, 2 * zl + r + 1] = silu(rms(v, g1[...])).astype(BF16)
            return 0

        lax.fori_loop(0, 8, one, 0)
        hx(s, 0).start()
        hx(s, 1).start()

    def convolve(s, i):
        for side in range(2):
            hx(s, side).wait_recv()
        top = hal[s, 0]
        bot = hal[s, 1]
        act[s, :, 0] = jnp.where(x > 0, top, jnp.zeros_like(top))
        act[s, :, 9] = jnp.where(x < 3, bot, jnp.zeros_like(bot))

        def one(grp, _):
            ys = []
            for dx in range(3):
                y = None
                for dy in range(3):
                    a = act[s, grp, dy : dy + 8].reshape(256, C)
                    m = dot(a, ws[dy, dx])
                    y = m if y is None else y + m
                ys.append(y)
            h = hid[grp * 4 + i].reshape(256, C) + ys[1]
            h = h + pltpu.roll(ys[0], 1, 0) + pltpu.roll(ys[2], 255, 0)
            hid[grp * 4 + i] = h.reshape(8, 32, C)
            act2[grp, 1 + i] = silu(rms(h, g2[...])).astype(BF16).reshape(8, 32, C)
            return 0

        lax.fori_loop(0, 2, one, 0)
        if i == 3:
            hf(0).start()
        if i == 0:
            hf(1).start()

    for s, i in enumerate(ORDER):
        activate(s, i)
        if s == 1:
            loads[0].wait()
        if s > 0:
            convolve(s - 1, ORDER[s - 1])
    convolve(3, ORDER[3])

    hf(0).wait_recv()
    hf(1).wait_recv()
    zero = jnp.zeros((8, 32, C), BF16)
    first, last = j == 0, j == 7
    act2[0, 0] = jnp.where(first, zero, edge[0, 0])
    act2[1, 0] = jnp.where(first, edge[0, 0], edge[0, 1])
    act2[0, 5] = jnp.where(last, edge[1, 1], edge[1, 0])
    act2[1, 5] = jnp.where(last, zero, edge[1, 1])
    loads[1].wait()

    def na(d):
        t = (j + d) % 8
        return remote(nsend.at[t], nrecv.at[j], sn.at[d], rn.at[d], dev_j(t))

    def temporal(k, _):
        r = (j + 1 + k) % 8
        total = None
        for t in range(3):
            a = act2[:, t : t + 4, r].reshape(256, C)
            m = dot(a, wt[t])
            total = m if total is None else total + m
        h = hid[:, r].reshape(256, C) + total
        hid[:, r] = h.reshape(8, 32, C)
        nsend[r] = rms(h, g3[...]).astype(BF16).reshape(8, 32, C)

        @pl.when(k < 7)
        def _():
            na(k + 1).start()

        return 0

    lax.fori_loop(0, 8, temporal, 0)
    nrecv[j] = nsend[j]
    for n in (2, 3, 4, 5):
        loads[n].wait()

    def project(d, _):
        src = (j + 8 - d) % 8

        @pl.when(d > 0)
        def _():
            remote(nsend.at[src], nrecv.at[src], sn.at[d], rn.at[d], dev_j(src)).wait_recv()

        a = nrecv[src].reshape(256, C)
        rows = pl.ds(pl.multiple_of(src * 256, 256), 256)
        for w, buf, scale in ((wq, qb, 0.125), (wk, kb, None), (wv, vb, None)):
            y = dot(a, w[...]).astype(BF16).astype(F32)
            y = y if scale is None else y * scale
            buf[0, rows, :] = y[:, 0:128]
            buf[1, rows, :] = y[:, 128:256]
            buf[2, rows, 0:D] = y[:, 256:320]
        return 0

    lax.fori_loop(0, 8, project, 0)

    low = lax.broadcasted_iota(jnp.int32, (64, 128), 1) < D

    def softmax_av(q, k, v):
        s = lax.dot_general(q, k, (((1,), (1,)), ((), ())), preferred_element_type=F32)
        e = jnp.exp(s - jnp.max(s, axis=-1, keepdims=True))
        tot = jnp.sum(e, axis=-1, keepdims=True)
        return dot(e.astype(BF16), v) / tot

    def pixel(p, _):
        rows = pl.ds(p, 64, stride=32)
        zq = jnp.zeros((64, 128), BF16)
        for hp in range(2):
            q = qb[hp, rows, :].astype(BF16)
            k = kb[hp, rows, :].astype(BF16)
            v = vb[hp, rows, :].astype(BF16)
            stacked = jnp.concatenate([jnp.where(low, q, zq), jnp.where(low, zq, q)], axis=0)
            o = softmax_av(stacked, k, v)
            ab[hp, rows, :] = jnp.where(low, o[:64], o[64:])
        q = qb[2, rows, :][:, :D].astype(BF16)
        k = kb[2, rows, :][:, :D].astype(BF16)
        v = vb[2, rows, :].astype(BF16)
        ab[2, rows, :] = softmax_av(q, k, v)
        return 0

    def aa(d, c):
        t = (j + d) % 8
        cols = pl.ds(c * 16, 16)
        return remote(asend.at[c, t], arecv.at[j, :, cols], sa.at[c, d], ra.at[c, d], dev_j(t))

    for c in range(2):
        lax.fori_loop(1 if c == 0 else 16, 16 if c == 0 else 31, pixel, 0)

        def gather(t, _):
            rows = pl.ds(pl.multiple_of(t * 256, 256), 256)
            full = jnp.concatenate([ab[0, rows, :], ab[1, rows, :], ab[2, rows, 0:D]], axis=-1)
            asend[c, t] = full.reshape(8, 32, C)[:, c * 16 : c * 16 + 16].astype(BF16)
            return 0

        lax.fori_loop(0, 8, gather, 0)
        for d in range(1, 8):
            aa(d, c).start()
        arecv[j, :, c * 16 : c * 16 + 16] = asend[c, j]

    for c in range(2):
        for d in range(1, 8):
            src = (j + 8 - d) % 8
            cols = pl.ds(c * 16, 16)
            remote(
                asend.at[c, src], arecv.at[src, :, cols], sa.at[c, d], ra.at[c, d], dev_j(src)
            ).wait_recv()

    def z2(k, i):
        t = (z + k) % 8
        return remote(zsend.at[t, i], out.at[z, i], sz.at[k, i], rz.at[k, i], dev_z(t))

    own = []
    for i in range(4):

        def finish(grp, _):
            a = arecv[:, grp * 4 + i].reshape(256, C)
            res = hid[grp * 4 + i].reshape(256, C) + dot(a, wo[...])
            res = res.reshape(4, 2, 32, C)
            for zl in range(4):
                zsend[grp * 4 + zl, i] = jnp.concatenate([res[zl, 0], res[zl, 1]], axis=-1).astype(BF16)
            return 0

        lax.fori_loop(0, 2, finish, 0)
        for k in range(1, 8):
            z2(k, i).start()
        cp = pltpu.make_async_copy(zsend.at[z, i], out.at[z, i], lsem.at[i])
        cp.start()
        own.append(cp)

    for i in range(4):
        own[i].wait()
        for k in range(1, 8):
            src = (z + 8 - k) % 8
            z1(k, i).wait_send()
            z2(k, i).wait_send()
            remote(zsend.at[src, i], out.at[src, i], sz.at[k, i], rz.at[k, i], dev_z(src)).wait_recv()
    for s in range(4):
        for side in range(2):
            hx(s, side).wait_send()
    for side in range(2):
        hf(side).wait_send()
    for d in range(1, 8):
        na(d).wait_send()
        for c in range(2):
            aa(d, c).wait_send()


def last_kernel(parts, out, tmp):
    for t in range(8):
        tmp[t] = parts[t, 0].astype(F32)
        both = tmp[t, 1:31, :]
        out[0, 0, 30 * t : 30 * t + 30, :] = both[:, 0:C]
        out[0, 1, 30 * t : 30 * t + 30, :] = both[:, C : 2 * C]


def local(latent, g1, ws, g2, wt, g3, wq, wk, wv, wo):
    vm = pl.BlockSpec(memory_space=pltpu.VMEM)
    anyspace = pl.BlockSpec(memory_space=pl.ANY)
    dma = pltpu.SemaphoreType.DMA
    parts = pl.pallas_call(
        main_kernel,
        out_shape=jax.ShapeDtypeStruct((8, 4, 32, 2 * C), BF16),
        in_specs=[vm] * 4 + [anyspace] * 6,
        out_specs=anyspace,
        scratch_shapes=[
            pltpu.VMEM((3, 3, C, C), BF16),
            pltpu.VMEM((3, C, C), BF16),
            pltpu.VMEM((C, C), BF16),
            pltpu.VMEM((C, C), BF16),
            pltpu.VMEM((C, C), BF16),
            pltpu.VMEM((C, C), BF16),
            pltpu.VMEM((256, 2 * C), F32),
            pltpu.VMEM((8, 4, 32, 2 * C), BF16),
            pltpu.VMEM((8, 4, 32, 2 * C), BF16),
            pltpu.VMEM((8, 8, 32, C), F32),
            pltpu.VMEM((4, 2, 10, 32, C), BF16),
            pltpu.VMEM((4, 2, 2, 32, C), BF16),
            pltpu.VMEM((2, 6, 8, 32, C), BF16),
            pltpu.VMEM((2, 2, 8, 32, C), BF16),
            pltpu.VMEM((8, 8, 32, C), BF16),
            pltpu.VMEM((8, 8, 32, C), BF16),
            pltpu.VMEM((3, 2048, 128), F32),
            pltpu.VMEM((3, 2048, 128), F32),
            pltpu.VMEM((3, 2048, 128), F32),
            pltpu.VMEM((3, 2048, 128), F32),
            pltpu.VMEM((2, 8, 8, 16, C), BF16),
            pltpu.VMEM((8, 8, 32, C), BF16),
            pltpu.VMEM((8, 4, 32, 2 * C), BF16),
            dma((6,)),
            dma((8, 4)), dma((8, 4)),
            dma((4, 2)), dma((4, 2)),
            dma((2,)), dma((2,)),
            dma((8,)), dma((8,)),
            dma((2, 8)), dma((2, 8)),
            dma((8, 4)), dma((8, 4)),
            dma((4,)),
        ],
        compiler_params=pltpu.CompilerParams(
            collective_id=0, has_side_effects=True, vmem_limit_bytes=60 * 1024 * 1024
        ),
        name="block",
    )(latent, g1.reshape(1, C), g2.reshape(1, C), g3.reshape(1, C), ws, wt, wq, wk, wv, wo)
    return pl.pallas_call(
        last_kernel,
        grid=(4,),
        out_shape=jax.ShapeDtypeStruct((4, 2, 240, C), F32),
        in_specs=[pl.BlockSpec((8, 1, 32, 2 * C), lambda i: (0, i, 0, 0))],
        out_specs=pl.BlockSpec((1, 2, 240, C), lambda i: (i, 0, 0, 0)),
        scratch_shapes=[pltpu.VMEM((8, 32, 2 * C), F32)],
        name="assemble",
    )(parts)


def solution(mesh):
    return jax.shard_map(
        local,
        mesh=mesh,
        in_specs=(P("frame", "row", None, None),) + (P(),) * 9,
        out_specs=P("frame", "row", None, None),
        check_vma=False,
    )
```

time: 397 us -> 149 us (0.38)
  the two profiles are of different devices: /device:TPU:63 before, /device:TPU:1 now
where the time goes in v2:
time: 149 us
  Pallas kernels  139 us (93%)
  local copies, waits for them, and re-layouts  9.65 us (6%)
    pallas_call x1, Pallas kernels, local(): pl.pallas_call(main_kernel, out_shape=jax.ShapeDtypeStruct((8, 4, 32, 2 *...  135 us
    pallas_call x1, Pallas kernels, local(): pl.pallas_call(last_kernel, grid=(4,), out_shape=jax.ShapeDtypeStruct((4,...  4.16 us
    pallas_call x1, local copies, waits for them, and re-layouts, local(): pl.pallas_call(last_kernel, grid=(4,), out_shape=jax.ShapeDtypeStruct((4,...  3.35 us

profile of v2, /device:TPU:1, one launch (start us, length us, event | category | flops | bytes accessed | tf_op | source)
XLA Modules:
  0.0 148.6 jit_solution(15485562146701434949)
XLA Ops:
  0.0 1.3 reshape.9.g1
  1.3 1.3 reshape.10.g2
  2.5 1.2 reshape.11.g3
  3.8 2.5 %copy.11.lat = bf16[4,2,240,320]{3,2,1,0:T(8,128)(2,1)} copy(bf16[4,2,240,320]{2,3,1,0:T(8,128)(2,1)} %param.10) | data formatting | bytes 2457600 | tf_op args[0]
  6.3 134.7 %block.1.parts = bf16[8,4,32,640]{3,2,1,0:T(8,128)(2,1)} custom-call(bf16[4,2,240,320]{3,2,1,0:T(8,128)(2,1)} %copy.11.lat, f32[1,320]{1,0:T(1,128)} %reshape.9.g1, f32[1,320]{1,0:T(1,128)} %reshape.10.g2, f32[1,320]{1,0:T(1,128)} %reshape.11.g3, bf16[3,3,320,320]{3,2,1,0:T(8,128)(2,1)} %ws_h.1, bf16[3,320,320]{2,1,0:T(8,128)(2,1)} %wt_h.1, ...), custom_call_target="tpu_custom_call" | custom-call | tf_op jit(solution)/shard_map/block/pallas_call | solution.py:316
  141.1 4.2 %assemble.1 = f32[4,2,240,320]{3,2,1,0:T(8,128)} custom-call(bf16[8,4,32,640]{3,2,1,0:T(8,128)(2,1)} %block.1.parts), custom_call_target="tpu_custom_call" | custom-call | tf_op jit(solution)/shard_map/assemble/pallas_call | solution.py:359
  145.2 3.4 %copy.12 = f32[4,2,240,320]{2,3,1,0:T(8,128)} copy(f32[4,2,240,320]{3,2,1,0:T(8,128)} %assemble.1) | data formatting | bytes 4915200 | tf_op jit(solution)/shard_map/assemble/pallas_call | solution.py:359

commit v3 on v2

--- a/solution.py
+++ b/solution.py
@@ -98,7 +98,7 @@
     def hf(side):
         t = (j + (7 if side else 1)) % 8
         slot = 1 if side else 4
-        return remote(act2.at[:, slot], edge.at[side], sf.at[side], rf.at[side], dev_j(t))
+        return remote(act2.at[:, :, slot], edge.at[side], sf.at[side], rf.at[side], dev_j(t))
 
     def activate(s, i):
         for k in range(1, 8):
@@ -110,7 +110,8 @@
             both = recv1[q, i].astype(F32)
             for r in range(2):
                 v = both[:, r * C : (r + 1) * C]
-                hid[grp * 4 + i, 2 * zl + r] = v
+                for c in range(2):
+                    hid[c, grp * 4 + i, 2 * zl + r] = v[c * 16 : c * 16 + 16]
                 act[s, grp, 2 * zl + r + 1] = silu(rms(v, g1[...])).astype(BF16)
             return 0
 
@@ -135,10 +136,12 @@
                     m = dot(a, ws[dy, dx])
                     y = m if y is None else y + m
                 ys.append(y)
-            h = hid[grp * 4 + i].reshape(256, C) + ys[1]
-            h = h + pltpu.roll(ys[0], 1, 0) + pltpu.roll(ys[2], 255, 0)
-            hid[grp * 4 + i] = h.reshape(8, 32, C)
-            act2[grp, 1 + i] = silu(rms(h, g2[...])).astype(BF16).reshape(8, 32, C)
+            y = ys[1] + pltpu.roll(ys[0], 1, 0) + pltpu.roll(ys[2], 255, 0)
+            y = y.reshape(8, 32, C)
+            for c in range(2):
+                h = hid[c, grp * 4 + i] + y[:, c * 16 : c * 16 + 16]
+                hid[c, grp * 4 + i] = h
+                act2[c, grp, 1 + i] = silu(rms(h, g2[...])).astype(BF16)
             return 0
 
         lax.fori_loop(0, 2, one, 0)
@@ -157,58 +160,60 @@
 
     hf(0).wait_recv()
     hf(1).wait_recv()
-    zero = jnp.zeros((8, 32, C), BF16)
+    zero = jnp.zeros((8, 16, C), BF16)
     first, last = j == 0, j == 7
-    act2[0, 0] = jnp.where(first, zero, edge[0, 0])
-    act2[1, 0] = jnp.where(first, edge[0, 0], edge[0, 1])
-    act2[0, 5] = jnp.where(last, edge[1, 1], edge[1, 0])
-    act2[1, 5] = jnp.where(last, zero, edge[1, 1])
+    for c in range(2):
+        act2[c, 0, 0] = jnp.where(first, zero, edge[0, c, 0])
+        act2[c, 1, 0] = jnp.where(first, edge[0, c, 0], edge[0, c, 1])
+        act2[c, 0, 5] = jnp.where(last, edge[1, c, 1], edge[1, c, 0])
+        act2[c, 1, 5] = jnp.where(last, zero, edge[1, c, 1])
     loads[1].wait()
 
-    def na(d):
+    def na(c, d):
         t = (j + d) % 8
-        return remote(nsend.at[t], nrecv.at[j], sn.at[d], rn.at[d], dev_j(t))
-
-    def temporal(k, _):
-        r = (j + 1 + k) % 8
+        return remote(nsend.at[c, t], nrecv.at[c, j], sn.at[c, d], rn.at[c, d], dev_j(t))
+
+    def temporal(c, kk):
+        pair = ((j + 1 + 2 * kk) % 8, (j + 2 + 2 * kk) % 8)
         total = None
         for t in range(3):
-            a = act2[:, t : t + 4, r].reshape(256, C)
+            a = jnp.concatenate([act2[c, :, t : t + 4, r].reshape(128, C) for r in pair], axis=0)
             m = dot(a, wt[t])
             total = m if total is None else total + m
-        h = hid[:, r].reshape(256, C) + total
-        hid[:, r] = h.reshape(8, 32, C)
-        nsend[r] = rms(h, g3[...]).astype(BF16).reshape(8, 32, C)
-
-        @pl.when(k < 7)
-        def _():
-            na(k + 1).start()
-
-        return 0
-
-    lax.fori_loop(0, 8, temporal, 0)
-    nrecv[j] = nsend[j]
+        for n, r in enumerate(pair):
+            h = hid[c, :, r].reshape(128, C) + total[n * 128 : n * 128 + 128]
+            hid[c, :, r] = h.reshape(8, 16, C)
+            nsend[c, r] = rms(h, g3[...]).astype(BF16).reshape(8, 16, C)
+            if 1 + 2 * kk + n < 8:
+                na(c, 1 + 2 * kk + n).start()
+
+    for c in range(2):
+        for kk in range(4):
+            temporal(c, kk)
+        nrecv[c, j] = nsend[c, j]
     for n in (2, 3, 4, 5):
         loads[n].wait()
 
-    def project(d, _):
-        src = (j + 8 - d) % 8
-
-        @pl.when(d > 0)
-        def _():
-            remote(nsend.at[src], nrecv.at[src], sn.at[d], rn.at[d], dev_j(src)).wait_recv()
-
-        a = nrecv[src].reshape(256, C)
-        rows = pl.ds(pl.multiple_of(src * 256, 256), 256)
-        for w, buf, scale in ((wq, qb, 0.125), (wk, kb, None), (wv, vb, None)):
-            y = dot(a, w[...]).astype(BF16).astype(F32)
-            y = y if scale is None else y * scale
-            buf[0, rows, :] = y[:, 0:128]
-            buf[1, rows, :] = y[:, 128:256]
-            buf[2, rows, 0:D] = y[:, 256:320]
-        return 0
-
-    lax.fori_loop(0, 8, project, 0)
+    def project(c):
+        for n in range(4):
+            pair = []
+            for d in (2 * n, 2 * n + 1):
+                src = (j + 8 - d) % 8
+                if d > 0:
+                    remote(
+                        nsend.at[c, src], nrecv.at[c, src], sn.at[c, d], rn.at[c, d], dev_j(src)
+                    ).wait_recv()
+                pair.append(src)
+            a = jnp.concatenate([nrecv[c, src].reshape(128, C) for src in pair], axis=0)
+            for w, buf, scale in ((wq, qb, 0.125), (wk, kb, None), (wv, vb, None)):
+                y = dot(a, w[...]).astype(BF16).astype(F32)
+                y = y if scale is None else y * scale
+                for m, src in enumerate(pair):
+                    rows = pl.ds(pl.multiple_of(c * 1024 + src * 128, 128), 128)
+                    part = y[m * 128 : m * 128 + 128]
+                    buf[0, rows, :] = part[:, 0:128]
+                    buf[1, rows, :] = part[:, 128:256]
+                    buf[2, rows, 0:D] = part[:, 256:320]
 
     low = lax.broadcasted_iota(jnp.int32, (64, 128), 1) < D
 
@@ -216,10 +221,10 @@
         s = lax.dot_general(q, k, (((1,), (1,)), ((), ())), preferred_element_type=F32)
         e = jnp.exp(s - jnp.max(s, axis=-1, keepdims=True))
         tot = jnp.sum(e, axis=-1, keepdims=True)
-        return dot(e.astype(BF16), v) / tot
-
-    def pixel(p, _):
-        rows = pl.ds(p, 64, stride=32)
+        return dot(e.astype(BF16), v) * (1.0 / tot)
+
+    def pixel(c, p):
+        rows = pl.ds(c * 1024 + p, 64, stride=16)
         zq = jnp.zeros((64, 128), BF16)
         for hp in range(2):
             q = qb[hp, rows, :].astype(BF16)
@@ -232,78 +237,84 @@
         k = kb[2, rows, :][:, :D].astype(BF16)
         v = vb[2, rows, :].astype(BF16)
         ab[2, rows, :] = softmax_av(q, k, v)
-        return 0
-
-    def aa(d, c):
+
+    def aa(c, d):
         t = (j + d) % 8
-        cols = pl.ds(c * 16, 16)
-        return remote(asend.at[c, t], arecv.at[j, :, cols], sa.at[c, d], ra.at[c, d], dev_j(t))
-
-    for c in range(2):
-        lax.fori_loop(1 if c == 0 else 16, 16 if c == 0 else 31, pixel, 0)
+        return remote(asend.at[c, t], arecv.at[c, j], sa.at[c, d], ra.at[c, d], dev_j(t))
+
+    def attend(c):
+        def five(n, _):
+            for m in range(5):
+                pixel(c, 1 - c + n * 5 + m)
+            return 0
+
+        lax.fori_loop(0, 3, five, 0)
 
         def gather(t, _):
-            rows = pl.ds(pl.multiple_of(t * 256, 256), 256)
+            rows = pl.ds(pl.multiple_of(c * 1024 + t * 128, 128), 128)
             full = jnp.concatenate([ab[0, rows, :], ab[1, rows, :], ab[2, rows, 0:D]], axis=-1)
-            asend[c, t] = full.reshape(8, 32, C)[:, c * 16 : c * 16 + 16].astype(BF16)
+            asend[c, t] = full.astype(BF16).reshape(8, 16, C)
             return 0
 
         lax.fori_loop(0, 8, gather, 0)
         for d in range(1, 8):
-            aa(d, c).start()
-        arecv[j, :, c * 16 : c * 16 + 16] = asend[c, j]
-
-    for c in range(2):
+            aa(c, d).start()
+        arecv[c, j] = asend[c, j]
+
+    def z2(c, k, i):
+        t = (z + k) % 8
+        return remote(zsend.at[c, t, i], out.at[c, z, i], sz.at[c, k, i], rz.at[c, k, i], dev_z(t))
+
+    def finish(c):
         for d in range(1, 8):
             src = (j + 8 - d) % 8
-            cols = pl.ds(c * 16, 16)
-            remote(
-                asend.at[c, src], arecv.at[src, :, cols], sa.at[c, d], ra.at[c, d], dev_j(src)
-            ).wait_recv()
-
-    def z2(k, i):
-        t = (z + k) % 8
-        return remote(zsend.at[t, i], out.at[z, i], sz.at[k, i], rz.at[k, i], dev_z(t))
-
-    own = []
+            remote(asend.at[c, src], arecv.at[c, src], sa.at[c, d], ra.at[c, d], dev_j(src)).wait_recv()
+        for i in range(4):
+            a = jnp.concatenate([arecv[c, :, g * 4 + i].reshape(128, C) for g in range(2)], axis=0)
+            mixed = dot(a, wo[...])
+            for g in range(2):
+                res = hid[c, g * 4 + i] + mixed[g * 128 : g * 128 + 128].reshape(8, 16, C)
+                for zl in range(4):
+                    both = jnp.concatenate([res[2 * zl], res[2 * zl + 1]], axis=-1)
+                    zsend[c, g * 4 + zl, i] = both.astype(BF16)
+            for k in range(1, 8):
+                z2(c, k, i).start()
+        cp = pltpu.make_async_copy(zsend.at[c, z], out.at[c, z], lsem.at[c])
+        cp.start()
+        return cp
+
+    project(0)
+    attend(0)
+    project(1)
+    attend(1)
+    own = [finish(0), finish(1)]
+
+    for c in range(2):
+        own[c].wait()
+        for i in range(4):
+            for k in range(1, 8):
+                src = (z + 8 - k) % 8
+                z2(c, k, i).wait_send()
+                remote(
+                    zsend.at[c, src, i], out.at[c, src, i], sz.at[c, k, i], rz.at[c, k, i], dev_z(src)
+                ).wait_recv()
+        for d in range(1, 8):
+            na(c, d).wait_send()
+            aa(c, d).wait_send()
     for i in range(4):
-
-        def finish(grp, _):
-            a = arecv[:, grp * 4 + i].reshape(256, C)
-            res = hid[grp * 4 + i].reshape(256, C) + dot(a, wo[...])
-            res = res.reshape(4, 2, 32, C)
-            for zl in range(4):
-                zsend[grp * 4 + zl, i] = jnp.concatenate([res[zl, 0], res[zl, 1]], axis=-1).astype(BF16)
-            return 0
-
-        lax.fori_loop(0, 2, finish, 0)
         for k in range(1, 8):
-            z2(k, i).start()
-        cp = pltpu.make_async_copy(zsend.at[z, i], out.at[z, i], lsem.at[i])
-        cp.start()
-        own.append(cp)
-
-    for i in range(4):
-        own[i].wait()
-        for k in range(1, 8):
-            src = (z + 8 - k) % 8
             z1(k, i).wait_send()
-            z2(k, i).wait_send()
-            remote(zsend.at[src, i], out.at[src, i], sz.at[k, i], rz.at[k, i], dev_z(src)).wait_recv()
     for s in range(4):
         for side in range(2):
             hx(s, side).wait_send()
     for side in range(2):
         hf(side).wait_send()
-    for d in range(1, 8):
-        na(d).wait_send()
-        for c in range(2):
-            aa(d, c).wait_send()
 
 
 def last_kernel(parts, out, tmp):
     for t in range(8):
-        tmp[t] = parts[t, 0].astype(F32)
+        tmp[t, 0:16] = parts[0, t, 0].astype(F32)
+        tmp[t, 16:32] = parts[1, t, 0].astype(F32)
         both = tmp[t, 1:31, :]
         out[0, 0, 30 * t : 30 * t + 30, :] = both[:, 0:C]
         out[0, 1, 30 * t : 30 * t + 30, :] = both[:, C : 2 * C]
@@ -315,7 +326,7 @@
     dma = pltpu.SemaphoreType.DMA
     parts = pl.pallas_call(
         main_kernel,
-        out_shape=jax.ShapeDtypeStruct((8, 4, 32, 2 * C), BF16),
+        out_shape=jax.ShapeDtypeStruct((2, 8, 4, 16, 2 * C), BF16),
         in_specs=[vm] * 4 + [anyspace] * 6,
         out_specs=anyspace,
         scratch_shapes=[
@@ -328,28 +339,28 @@
             pltpu.VMEM((256, 2 * C), F32),
             pltpu.VMEM((8, 4, 32, 2 * C), BF16),
             pltpu.VMEM((8, 4, 32, 2 * C), BF16),
-            pltpu.VMEM((8, 8, 32, C), F32),
+            pltpu.VMEM((2, 8, 8, 16, C), F32),
             pltpu.VMEM((4, 2, 10, 32, C), BF16),
             pltpu.VMEM((4, 2, 2, 32, C), BF16),
-            pltpu.VMEM((2, 6, 8, 32, C), BF16),
-            pltpu.VMEM((2, 2, 8, 32, C), BF16),
-            pltpu.VMEM((8, 8, 32, C), BF16),
-            pltpu.VMEM((8, 8, 32, C), BF16),
+            pltpu.VMEM((2, 2, 6, 8, 16, C), BF16),
+            pltpu.VMEM((2, 2, 2, 8, 16, C), BF16),
+            pltpu.VMEM((2, 8, 8, 16, C), BF16),
+            pltpu.VMEM((2, 8, 8, 16, C), BF16),
             pltpu.VMEM((3, 2048, 128), F32),
             pltpu.VMEM((3, 2048, 128), F32),
             pltpu.VMEM((3, 2048, 128), F32),
             pltpu.VMEM((3, 2048, 128), F32),
             pltpu.VMEM((2, 8, 8, 16, C), BF16),
-            pltpu.VMEM((8, 8, 32, C), BF16),
-            pltpu.VMEM((8, 4, 32, 2 * C), BF16),
+            pltpu.VMEM((2, 8, 8, 16, C), BF16),
+            pltpu.VMEM((2, 8, 4, 16, 2 * C), BF16),
             dma((6,)),
             dma((8, 4)), dma((8, 4)),
             dma((4, 2)), dma((4, 2)),
             dma((2,)), dma((2,)),
-            dma((8,)), dma((8,)),
             dma((2, 8)), dma((2, 8)),
-            dma((8, 4)), dma((8, 4)),
-            dma((4,)),
+            dma((2, 8)), dma((2, 8)),
+            dma((2, 8, 4)), dma((2, 8, 4)),
+            dma((2,)),
         ],
         compiler_params=pltpu.CompilerParams(
             collective_id=0, has_side_effects=True, vmem_limit_bytes=60 * 1024 * 1024
@@ -360,7 +371,7 @@
         last_kernel,
         grid=(4,),
         out_shape=jax.ShapeDtypeStruct((4, 2, 240, C), F32),
-        in_specs=[pl.BlockSpec((8, 1, 32, 2 * C), lambda i: (0, i, 0, 0))],
+        in_specs=[pl.BlockSpec((2, 8, 1, 16, 2 * C), lambda i: (0, 0, i, 0, 0))],
         out_specs=pl.BlockSpec((1, 2, 240, C), lambda i: (i, 0, 0, 0)),
         scratch_shapes=[pltpu.VMEM((8, 32, 2 * C), F32)],
         name="assemble",

time: 149 us -> 128 us (0.86)
  Pallas kernels: 139 us -> 118 us
    pallas_call x1, Pallas kernels: 135 us -> 113 us  [local(): pl.pallas_call(main_kernel, out_shape=jax.ShapeDtypeStruct((2, 8, 4, 16,...]
where the time goes in v3:
time: 128 us; the launch traced here: 127 us
  Pallas kernels  118 us (92%)
  local copies, waits for them, and re-layouts  9.65 us (8%)
    pallas_call x1, Pallas kernels, local(): pl.pallas_call(main_kernel, out_shape=jax.ShapeDtypeStruct((2, 8, 4, 16,...  113 us
    pallas_call x1, Pallas kernels, local(): pl.pallas_call(last_kernel, grid=(4,), out_shape=jax.ShapeDtypeStruct((4,...  4.16 us
    pallas_call x1, local copies, waits for them, and re-layouts, local(): pl.pallas_call(last_kernel, grid=(4,), out_shape=jax.ShapeDtypeStruct((4,...  3.35 us

profile of v3, /device:TPU:1, one launch (start us, length us, event | category | flops | bytes accessed | tf_op | source)
XLA Modules:
  0.0 127.3 jit_solution(14556115302619186329)
XLA Ops:
  0.0 1.3 reshape.9.g1
  1.3 1.3 reshape.10.g2
  2.5 1.2 reshape.11.g3
  3.8 2.5 %copy.11.lat = bf16[4,2,240,320]{3,2,1,0:T(8,128)(2,1)} copy(bf16[4,2,240,320]{2,3,1,0:T(8,128)(2,1)} %param.10) | data formatting | bytes 2457600 | tf_op args[0]
  6.3 113.4 %block.1.parts = bf16[2,8,4,16,640]{4,3,2,1,0:T(8,128)(2,1)} custom-call(bf16[4,2,240,320]{3,2,1,0:T(8,128)(2,1)} %copy.11.lat, f32[1,320]{1,0:T(1,128)} %reshape.9.g1, f32[1,320]{1,0:T(1,128)} %reshape.10.g2, f32[1,320]{1,0:T(1,128)} %reshape.11.g3, bf16[3,3,320,320]{3,2,1,0:T(8,128)(2,1)} %ws_h.1, bf16[3,320,320]{2,1,0:T(8,128)(2,1)} %wt_h.1, ...), custom_call_target="tpu_custom_call" | custom-call | tf_op jit(solution)/shard_map/block/pallas_call | solution.py:327
  119.8 4.2 %assemble.1 = f32[4,2,240,320]{3,2,1,0:T(8,128)} custom-call(bf16[2,8,4,16,640]{4,3,2,1,0:T(8,128)(2,1)} %block.1.parts), custom_call_target="tpu_custom_call" | custom-call | tf_op jit(solution)/shard_map/assemble/pallas_call | solution.py:370
  123.9 3.4 %copy.12 = f32[4,2,240,320]{2,3,1,0:T(8,128)} copy(f32[4,2,240,320]{3,2,1,0:T(8,128)} %assemble.1) | data formatting | bytes 4915200 | tf_op jit(solution)/shard_map/assemble/pallas_call | solution.py:370

commit v4 on v3

--- a/solution.py
+++ b/solution.py
@@ -70,104 +70,126 @@
     def remote(src, dst, ss, rs, dev):
         return pltpu.make_async_remote_copy(src, dst, ss, rs, device_id=dev, device_id_type=MESH)
 
-    def z1(k, i):
+    def z1(c, k, i):
         t = (z + k) % 8
-        return remote(send1.at[t, i], recv1.at[z, i], s1.at[k, i], r1.at[k, i], dev_z(t))
+        return remote(send1.at[c, t, i], recv1.at[c, z, i], s1.at[c, k, i], r1.at[c, k, i], dev_z(t))
 
     pad[0:8] = jnp.zeros((8, 2 * C), F32)
     pad[248:256] = jnp.zeros((8, 2 * C), F32)
     for n, i in enumerate(ORDER):
         pad[8:248, 0:C] = lat[i, 0].astype(F32)
         pad[8:248, C : 2 * C] = lat[i, 1].astype(F32)
-
         for t in range(8):
-            send1[t, i] = pad[7 + 30 * t : 39 + 30 * t, :].astype(BF16)
+            for c in range(2):
+                lo = 7 + 30 * t + 16 * c
+                send1[c, t, i] = pad[lo : lo + 16, :].astype(BF16)
         if n == 0:
             pl.semaphore_wait(bar, 16)
         for k in range(1, 8):
-            z1(k, i).start()
-        recv1[z, i] = send1[z, i]
-
-    def hx(s, side):
+            z1(0, k, i).start()
+        for c in range(2):
+            recv1[c, z, i] = send1[c, z, i]
+    for i in ORDER:
+        for k in range(1, 8):
+            z1(1, k, i).start()
+
+    def hx(c, s, side):
         t = (x + (3 if side else 1)) % 4
         row = 1 if side else 8
         return remote(
-            act.at[s, :, row], hal.at[s, side], sx.at[s, side], rx.at[s, side], dev_x(t)
+            act.at[s, :, row, pl.ds(c * 16, 16)],
+            hal.at[c, s, side],
+            sx.at[c, s, side],
+            rx.at[c, s, side],
+            dev_x(t),
         )
 
-    def hf(side):
+    def hf(c, side):
         t = (j + (7 if side else 1)) % 8
         slot = 1 if side else 4
-        return remote(act2.at[:, :, slot], edge.at[side], sf.at[side], rf.at[side], dev_j(t))
-
-    def activate(s, i):
+        return remote(
+            act2.at[c, :, slot], edge.at[side, c], sf.at[c, side], rf.at[c, side], dev_j(t)
+        )
+
+    def activate(c, s, i):
         for k in range(1, 8):
             src = (z + 8 - k) % 8
-            remote(send1.at[src, i], recv1.at[src, i], s1.at[k, i], r1.at[k, i], dev_z(src)).wait_recv()
+            remote(
+                send1.at[c, src, i], recv1.at[c, src, i], s1.at[c, k, i], r1.at[c, k, i], dev_z(src)
+            ).wait_recv()
 
         def one(q, _):
             grp, zl = q // 4, q % 4
-            both = recv1[q, i].astype(F32)
+            both = recv1[c, q, i].astype(F32)
+            if c == 1:
+                before = recv1[0, q, i].astype(F32)
             for r in range(2):
                 v = both[:, r * C : (r + 1) * C]
-                for c in range(2):
-                    hid[c, grp * 4 + i, 2 * zl + r] = v[c * 16 : c * 16 + 16]
-                act[s, grp, 2 * zl + r + 1] = silu(rms(v, g1[...])).astype(BF16)
+                kept = v
+                if c == 1:
+                    kept = jnp.where(tail, before[:, r * C : (r + 1) * C], v)
+                hid[c, grp * 4 + i, 2 * zl + r] = kept
+                act[s, grp, 2 * zl + r + 1, c * 16 : c * 16 + 16] = silu(rms(v, g1[...])).astype(BF16)
             return 0
 
         lax.fori_loop(0, 8, one, 0)
-        hx(s, 0).start()
-        hx(s, 1).start()
-
-    def convolve(s, i):
+        hx(c, s, 0).start()
+        hx(c, s, 1).start()
+
+    tail = lax.broadcasted_iota(jnp.int32, (16, C), 0) == 15
+    tail8 = lax.broadcasted_iota(jnp.int32, (8, 16, C), 1) == 15
+
+    def convolve(c, s, i):
         for side in range(2):
-            hx(s, side).wait_recv()
-        top = hal[s, 0]
-        bot = hal[s, 1]
-        act[s, :, 0] = jnp.where(x > 0, top, jnp.zeros_like(top))
-        act[s, :, 9] = jnp.where(x < 3, bot, jnp.zeros_like(bot))
-
-        def one(grp, _):
+            hx(c, s, side).wait_recv()
+        cols = slice(c * 16, c * 16 + 16)
+        top = hal[c, s, 0]
+        bot = hal[c, s, 1]
+        act[s, :, 0, cols] = jnp.where(x > 0, top, jnp.zeros_like(top))
+        act[s, :, 9, cols] = jnp.where(x < 3, bot, jnp.zeros_like(bot))
+
+        def mix(read):
             ys = []
             for dx in range(3):
                 y = None
                 for dy in range(3):
-                    a = act[s, grp, dy : dy + 8].reshape(256, C)
-                    m = dot(a, ws[dy, dx])
+                    m = dot(read(dy), ws[dy, dx])
                     y = m if y is None else y + m
                 ys.append(y)
-            y = ys[1] + pltpu.roll(ys[0], 1, 0) + pltpu.roll(ys[2], 255, 0)
-            y = y.reshape(8, 32, C)
-            for c in range(2):
-                h = hid[c, grp * 4 + i] + y[:, c * 16 : c * 16 + 16]
-                hid[c, grp * 4 + i] = h
-                act2[c, grp, 1 + i] = silu(rms(h, g2[...])).astype(BF16)
-            return 0
-
-        lax.fori_loop(0, 2, one, 0)
+            return ys[1] + pltpu.roll(ys[0], 1, 0) + pltpu.roll(ys[2], 255, 0)
+
+        def close(grp, y):
+            h = hid[c, grp * 4 + i] + y
+            hid[c, grp * 4 + i] = h
+            act2[c, grp, 1 + i] = silu(rms(h, g2[...])).astype(BF16)
+
+        if c == 0:
+            y = mix(lambda dy: act[s, :, dy : dy + 8, 0:16].reshape(256, C))
+            for grp in range(2):
+                close(grp, y[grp * 128 : grp * 128 + 128].reshape(8, 16, C))
+        else:
+
+            def one(grp, _):
+                y = mix(lambda dy: act[s, grp, dy : dy + 8].reshape(256, C)).reshape(8, 32, C)
+                close(grp, jnp.where(tail8, y[:, 0:16], y[:, 16:32]))
+                return 0
+
+            lax.fori_loop(0, 2, one, 0)
         if i == 3:
-            hf(0).start()
+            hf(c, 0).start()
         if i == 0:
-            hf(1).start()
-
-    for s, i in enumerate(ORDER):
-        activate(s, i)
-        if s == 1:
-            loads[0].wait()
-        if s > 0:
-            convolve(s - 1, ORDER[s - 1])
-    convolve(3, ORDER[3])
-
-    hf(0).wait_recv()
-    hf(1).wait_recv()
+            hf(c, 1).start()
+
     zero = jnp.zeros((8, 16, C), BF16)
     first, last = j == 0, j == 7
-    for c in range(2):
+
+    def border(c):
+        hf(c, 0).wait_recv()
+        hf(c, 1).wait_recv()
         act2[c, 0, 0] = jnp.where(first, zero, edge[0, c, 0])
         act2[c, 1, 0] = jnp.where(first, edge[0, c, 0], edge[0, c, 1])
         act2[c, 0, 5] = jnp.where(last, edge[1, c, 1], edge[1, c, 0])
         act2[c, 1, 5] = jnp.where(last, zero, edge[1, c, 1])
-    loads[1].wait()
 
     def na(c, d):
         t = (j + d) % 8
@@ -188,6 +210,16 @@
                 na(c, 1 + 2 * kk + n).start()
 
     for c in range(2):
+        for s, i in enumerate(ORDER):
+            activate(c, s, i)
+            if c == 0 and s == 1:
+                loads[0].wait()
+            if s > 0:
+                convolve(c, s - 1, ORDER[s - 1])
+        convolve(c, 3, ORDER[3])
+        border(c)
+        if c == 0:
+            loads[1].wait()
         for kk in range(4):
             temporal(c, kk)
         nrecv[c, j] = nsend[c, j]
@@ -243,12 +275,14 @@
         return remote(asend.at[c, t], arecv.at[c, j], sa.at[c, d], ra.at[c, d], dev_j(t))
 
     def attend(c):
-        def five(n, _):
-            for m in range(5):
-                pixel(c, 1 - c + n * 5 + m)
+        step = 4 if c else 7
+
+        def several(n, _):
+            for m in range(step):
+                pixel(c, 1 - c + n * step + m)
             return 0
 
-        lax.fori_loop(0, 3, five, 0)
+        lax.fori_loop(0, 4 if c else 2, several, 0)
 
         def gather(t, _):
             rows = pl.ds(pl.multiple_of(c * 1024 + t * 128, 128), 128)
@@ -301,20 +335,22 @@
         for d in range(1, 8):
             na(c, d).wait_send()
             aa(c, d).wait_send()
-    for i in range(4):
-        for k in range(1, 8):
-            z1(k, i).wait_send()
-    for s in range(4):
+    for c in range(2):
+        for i in range(4):
+            for k in range(1, 8):
+                z1(c, k, i).wait_send()
         for side in range(2):
-            hx(s, side).wait_send()
-    for side in range(2):
-        hf(side).wait_send()
+            for s in range(4):
+                hx(c, s, side).wait_send()
+            hf(c, side).wait_send()
 
 
 def last_kernel(parts, out, tmp):
+    tail = lax.broadcasted_iota(jnp.int32, (16, 2 * C), 0) == 15
     for t in range(8):
-        tmp[t, 0:16] = parts[0, t, 0].astype(F32)
-        tmp[t, 16:32] = parts[1, t, 0].astype(F32)
+        right = parts[1, t, 0].astype(F32)
+        tmp[t, 0:16] = jnp.where(tail, right, parts[0, t, 0].astype(F32))
+        tmp[t, 16:32] = right
         both = tmp[t, 1:31, :]
         out[0, 0, 30 * t : 30 * t + 30, :] = both[:, 0:C]
         out[0, 1, 30 * t : 30 * t + 30, :] = both[:, C : 2 * C]
@@ -337,11 +373,11 @@
             pltpu.VMEM((C, C), BF16),
             pltpu.VMEM((C, C), BF16),
             pltpu.VMEM((256, 2 * C), F32),
-            pltpu.VMEM((8, 4, 32, 2 * C), BF16),
-            pltpu.VMEM((8, 4, 32, 2 * C), BF16),
+            pltpu.VMEM((2, 8, 4, 16, 2 * C), BF16),
+            pltpu.VMEM((2, 8, 4, 16, 2 * C), BF16),
             pltpu.VMEM((2, 8, 8, 16, C), F32),
             pltpu.VMEM((4, 2, 10, 32, C), BF16),
-            pltpu.VMEM((4, 2, 2, 32, C), BF16),
+            pltpu.VMEM((2, 4, 2, 2, 16, C), BF16),
             pltpu.VMEM((2, 2, 6, 8, 16, C), BF16),
             pltpu.VMEM((2, 2, 2, 8, 16, C), BF16),
             pltpu.VMEM((2, 8, 8, 16, C), BF16),
@@ -354,9 +390,9 @@
             pltpu.VMEM((2, 8, 8, 16, C), BF16),
             pltpu.VMEM((2, 8, 4, 16, 2 * C), BF16),
             dma((6,)),
-            dma((8, 4)), dma((8, 4)),
-            dma((4, 2)), dma((4, 2)),
-            dma((2,)), dma((2,)),
+            dma((2, 8, 4)), dma((2, 8, 4)),
+            dma((2, 4, 2)), dma((2, 4, 2)),
+            dma((2, 2)), dma((2, 2)),
             dma((2, 8)), dma((2, 8)),
             dma((2, 8)), dma((2, 8)),
             dma((2, 8, 4)), dma((2, 8, 4)),

time: 128 us -> 128 us (level)
  no operation moved by 1% of the time
where the time goes in v4:
time: 128 us; the launch traced here: 127 us
  Pallas kernels  118 us (92%)
  local copies, waits for them, and re-layouts  9.65 us (8%)
    pallas_call x1, Pallas kernels, local(): pl.pallas_call(main_kernel, out_shape=jax.ShapeDtypeStruct((2, 8, 4, 16,...  113 us
    pallas_call x1, Pallas kernels, local(): pl.pallas_call(last_kernel, grid=(4,), out_shape=jax.ShapeDtypeStruct((4,...  4.16 us
    pallas_call x1, local copies, waits for them, and re-layouts, local(): pl.pallas_call(last_kernel, grid=(4,), out_shape=jax.ShapeDtypeStruct((4,...  3.35 us

profile of v4, /device:TPU:1, one launch (start us, length us, event | category | flops | bytes accessed | tf_op | source)
XLA Modules:
  0.0 127.3 jit_solution(9861440392769631655)
XLA Ops:
  0.0 1.3 reshape.9.g1
  1.3 1.3 reshape.10.g2
  2.5 1.2 reshape.11.g3
  3.8 2.5 %copy.11.lat = bf16[4,2,240,320]{3,2,1,0:T(8,128)(2,1)} copy(bf16[4,2,240,320]{2,3,1,0:T(8,128)(2,1)} %param.10) | data formatting | bytes 2457600 | tf_op args[0]
  6.3 113.4 %block.1.parts = bf16[2,8,4,16,640]{4,3,2,1,0:T(8,128)(2,1)} custom-call(bf16[4,2,240,320]{3,2,1,0:T(8,128)(2,1)} %copy.11.lat, f32[1,320]{1,0:T(1,128)} %reshape.9.g1, f32[1,320]{1,0:T(1,128)} %reshape.10.g2, f32[1,320]{1,0:T(1,128)} %reshape.11.g3, bf16[3,3,320,320]{3,2,1,0:T(8,128)(2,1)} %ws_h.1, bf16[3,320,320]{2,1,0:T(8,128)(2,1)} %wt_h.1, ...), custom_call_target="tpu_custom_call" | custom-call | tf_op jit(solution)/shard_map/block/pallas_call | solution.py:363
  119.7 4.2 %assemble.1 = f32[4,2,240,320]{3,2,1,0:T(8,128)} custom-call(bf16[2,8,4,16,640]{4,3,2,1,0:T(8,128)(2,1)} %block.1.parts), custom_call_target="tpu_custom_call" | custom-call | tf_op jit(solution)/shard_map/assemble/pallas_call | solution.py:406
  123.9 3.4 %copy.12 = f32[4,2,240,320]{2,3,1,0:T(8,128)} copy(f32[4,2,240,320]{3,2,1,0:T(8,128)} %assemble.1) | data formatting | bytes 4915200 | tf_op jit(solution)/shard_map/assemble/pallas_call | solution.py:406

commit v5 on v4

--- a/solution.py
+++ b/solution.py
@@ -21,7 +21,8 @@
 
 
 def silu(v):
-    return v / (1.0 + jnp.exp(-v))
+    half = 0.5 * v
+    return half + half * jnp.tanh(half)
 
 
 def dot(a, b):
@@ -33,7 +34,7 @@
     out,
     ws, wt, wq, wk, wv, wo,
     pad, send1, recv1, hid, act, hal, act2, edge, nsend, nrecv,
-    qb, kb, vb, ab, asend, arecv, zsend,
+    qb, kb, vb, ab, asend, arecv, zsend, keep,
     wsem, s1, r1, sx, rx, sf, rf, sn, rn, sa, ra, sz, rz, lsem,
 ):
     me_f = lax.axis_index("frame")
@@ -137,7 +138,6 @@
         hx(c, s, 1).start()
 
     tail = lax.broadcasted_iota(jnp.int32, (16, C), 0) == 15
-    tail8 = lax.broadcasted_iota(jnp.int32, (8, 16, C), 1) == 15
 
     def convolve(c, s, i):
         for side in range(2):
@@ -156,25 +156,26 @@
                     m = dot(read(dy), ws[dy, dx])
                     y = m if y is None else y + m
                 ys.append(y)
-            return ys[1] + pltpu.roll(ys[0], 1, 0) + pltpu.roll(ys[2], 255, 0)
+            return ys
 
         def close(grp, y):
             h = hid[c, grp * 4 + i] + y
             hid[c, grp * 4 + i] = h
             act2[c, grp, 1 + i] = silu(rms(h, g2[...])).astype(BF16)
 
+        y0, y1, y2 = mix(lambda dy: act[s, :, dy : dy + 8, cols].reshape(256, C))
         if c == 0:
-            y = mix(lambda dy: act[s, :, dy : dy + 8, 0:16].reshape(256, C))
-            for grp in range(2):
-                close(grp, y[grp * 128 : grp * 128 + 128].reshape(8, 16, C))
+            part = y1 + pltpu.roll(y0, 1, 0)
+            keep[s, 0] = y0
+            keep[s, 1] = part
+            y = part + pltpu.roll(y2, 255, 0)
         else:
-
-            def one(grp, _):
-                y = mix(lambda dy: act[s, grp, dy : dy + 8].reshape(256, C)).reshape(8, 32, C)
-                close(grp, jnp.where(tail8, y[:, 0:16], y[:, 16:32]))
-                return 0
-
-            lax.fori_loop(0, 2, one, 0)
+            slot = lax.broadcasted_iota(jnp.int32, (256, C), 0) % 16
+            left = jnp.where(slot == 0, pltpu.roll(keep[s, 0], 241, 0), pltpu.roll(y0, 1, 0))
+            y = y1 + left + pltpu.roll(y2, 255, 0)
+            y = jnp.where(slot == 15, keep[s, 1] + pltpu.roll(y2, 15, 0), y)
+        for grp in range(2):
+            close(grp, y[grp * 128 : grp * 128 + 128].reshape(8, 16, C))
         if i == 3:
             hf(c, 0).start()
         if i == 0:
@@ -389,6 +390,7 @@
             pltpu.VMEM((2, 8, 8, 16, C), BF16),
             pltpu.VMEM((2, 8, 8, 16, C), BF16),
             pltpu.VMEM((2, 8, 4, 16, 2 * C), BF16),
+            pltpu.VMEM((4, 2, 256, C), F32),
             dma((6,)),
             dma((2, 8, 4)), dma((2, 8, 4)),
             dma((2, 4, 2)), dma((2, 4, 2)),

time: 128 us -> 124 us (0.969)
  Pallas kernels: 118 us -> 113 us
    pallas_call x1, Pallas kernels: 113 us -> 109 us  [local(): pl.pallas_call(main_kernel, out_shape=jax.ShapeDtypeStruct((2, 8, 4, 16,...]
where the time goes in v5:
time: 124 us; the launch traced here: 122 us
  Pallas kernels  113 us (91%)
  local copies, waits for them, and re-layouts  9.65 us (8%)
    pallas_call x1, Pallas kernels, local(): pl.pallas_call(main_kernel, out_shape=jax.ShapeDtypeStruct((2, 8, 4, 16,...  109 us
    pallas_call x1, Pallas kernels, local(): pl.pallas_call(last_kernel, grid=(4,), out_shape=jax.ShapeDtypeStruct((4,...  4.16 us
    pallas_call x1, local copies, waits for them, and re-layouts, local(): pl.pallas_call(last_kernel, grid=(4,), out_shape=jax.ShapeDtypeStruct((4,...  3.35 us
    unnamed x1, local copies, waits for them, and re-layouts  2.51 us

profile of v5, /device:TPU:1, one launch (start us, length us, event | category | flops | bytes accessed | tf_op | source)
XLA Modules:
  0.0 122.4 jit_solution(12012289466421391720)
XLA Ops:
  0.0 1.3 %reshape.9.g1 = f32[1,320]{1,0:T(1,128)} reshape(f32[320]{0:T(512)} %param.11) | data formatting | bytes 2560 | tf_op jit(solution)/shard_map/reshape | solution.py:407
  1.3 1.3 %reshape.10.g2 = f32[1,320]{1,0:T(1,128)} reshape(f32[320]{0:T(512)} %param.13) | data formatting | bytes 2560 | tf_op jit(solution)/shard_map/reshape | solution.py:407
  2.5 1.2 %reshape.11.g3 = f32[1,320]{1,0:T(1,128)} reshape(f32[320]{0:T(512)} %param.15) | data formatting | bytes 2560 | tf_op jit(solution)/shard_map/reshape | solution.py:407
  3.8 2.5 %copy.11.lat = bf16[4,2,240,320]{3,2,1,0:T(8,128)(2,1)} copy(bf16[4,2,240,320]{2,3,1,0:T(8,128)(2,1)} %param.10) | data formatting | bytes 2457600 | tf_op args[0]
  6.3 108.6 %block.1.parts = bf16[2,8,4,16,640]{4,3,2,1,0:T(8,128)(2,1)} custom-call(bf16[4,2,240,320]{3,2,1,0:T(8,128)(2,1)} %copy.11.lat, f32[1,320]{1,0:T(1,128)} %reshape.9.g1, f32[1,320]{1,0:T(1,128)} %reshape.10.g2, f32[1,320]{1,0:T(1,128)} %reshape.11.g3, bf16[3,3,320,320]{3,2,1,0:T(8,128)(2,1)} %ws_h.1, bf16[3,320,320]{2,1,0:T(8,128)(2,1)} %wt_h.1, ...), custom_call_target="tpu_custom_call" | custom-call | tf_op jit(solution)/shard_map/block/pallas_call | solution.py:364
  114.9 4.2 %assemble.1 = f32[4,2,240,320]{3,2,1,0:T(8,128)} custom-call(bf16[2,8,4,16,640]{4,3,2,1,0:T(8,128)(2,1)} %block.1.parts), custom_call_target="tpu_custom_call" | custom-call | tf_op jit(solution)/shard_map/assemble/pallas_call | solution.py:408
  119.1 3.4 %copy.12 = f32[4,2,240,320]{2,3,1,0:T(8,128)} copy(f32[4,2,240,320]{3,2,1,0:T(8,128)} %assemble.1) | data formatting | bytes 4915200 | tf_op jit(solution)/shard_map/assemble/pallas_call | solution.py:408

commit v6 on v5

--- a/solution.py
+++ b/solution.py
@@ -209,23 +209,6 @@
             nsend[c, r] = rms(h, g3[...]).astype(BF16).reshape(8, 16, C)
             if 1 + 2 * kk + n < 8:
                 na(c, 1 + 2 * kk + n).start()
-
-    for c in range(2):
-        for s, i in enumerate(ORDER):
-            activate(c, s, i)
-            if c == 0 and s == 1:
-                loads[0].wait()
-            if s > 0:
-                convolve(c, s - 1, ORDER[s - 1])
-        convolve(c, 3, ORDER[3])
-        border(c)
-        if c == 0:
-            loads[1].wait()
-        for kk in range(4):
-            temporal(c, kk)
-        nrecv[c, j] = nsend[c, j]
-    for n in (2, 3, 4, 5):
-        loads[n].wait()
 
     def project(c):
         for n in range(4):
@@ -318,11 +301,30 @@
         cp.start()
         return cp
 
-    project(0)
-    attend(0)
+    for c in range(2):
+        for s, i in enumerate(ORDER):
+            activate(c, s, i)
+            if c == 0 and s == 1:
+                loads[0].wait()
+            if s > 0:
+                convolve(c, s - 1, ORDER[s - 1])
+        convolve(c, 3, ORDER[3])
+        if c == 1:
+            for n in (2, 3, 4, 5):
+                loads[n].wait()
+            project(0)
+            attend(0)
+        border(c)
+        if c == 0:
+            loads[1].wait()
+        for kk in range(4):
+            temporal(c, kk)
+        nrecv[c, j] = nsend[c, j]
+
+    own = [finish(0)]
     project(1)
     attend(1)
-    own = [finish(0), finish(1)]
+    own.append(finish(1))
 
     for c in range(2):
         own[c].wait()

time: 124 us -> 131 us (1.056)
  Pallas kernels: 113 us -> 121 us
    pallas_call x1, Pallas kernels: 109 us -> 117 us  [local(): pl.pallas_call(main_kernel, out_shape=jax.ShapeDtypeStruct((2, 8, 4, 16,...]
where the time goes in v6:
time: 131 us
  Pallas kernels  121 us (92%)
  local copies, waits for them, and re-layouts  9.65 us (7%)
    pallas_call x1, Pallas kernels, local(): pl.pallas_call(main_kernel, out_shape=jax.ShapeDtypeStruct((2, 8, 4, 16,...  117 us
    pallas_call x1, Pallas kernels, local(): pl.pallas_call(last_kernel, grid=(4,), out_shape=jax.ShapeDtypeStruct((4,...  4.16 us
    pallas_call x1, local copies, waits for them, and re-layouts, local(): pl.pallas_call(last_kernel, grid=(4,), out_shape=jax.ShapeDtypeStruct((4,...  3.35 us

profile of v6, /device:TPU:1, one launch (start us, length us, event | category | flops | bytes accessed | tf_op | source)
XLA Modules:
  0.0 130.7 jit_solution(9601566688708879814)
XLA Ops:
  0.0 1.3 reshape.9.g1
  1.3 1.3 reshape.10.g2
  2.5 1.2 reshape.11.g3
  3.8 2.5 %copy.11.lat = bf16[4,2,240,320]{3,2,1,0:T(8,128)(2,1)} copy(bf16[4,2,240,320]{2,3,1,0:T(8,128)(2,1)} %param.10) | data formatting | bytes 2457600 | tf_op args[0]
  6.3 116.8 %block.1.parts = bf16[2,8,4,16,640]{4,3,2,1,0:T(8,128)(2,1)} custom-call(bf16[4,2,240,320]{3,2,1,0:T(8,128)(2,1)} %copy.11.lat, f32[1,320]{1,0:T(1,128)} %reshape.9.g1, f32[1,320]{1,0:T(1,128)} %reshape.10.g2, f32[1,320]{1,0:T(1,128)} %reshape.11.g3, bf16[3,3,320,320]{3,2,1,0:T(8,128)(2,1)} %ws_h.1, bf16[3,320,320]{2,1,0:T(8,128)(2,1)} %wt_h.1, ...), custom_call_target="tpu_custom_call" | custom-call | tf_op jit(solution)/shard_map/block/pallas_call | solution.py:366
  123.1 4.2 %assemble.1 = f32[4,2,240,320]{3,2,1,0:T(8,128)} custom-call(bf16[2,8,4,16,640]{4,3,2,1,0:T(8,128)(2,1)} %block.1.parts), custom_call_target="tpu_custom_call" | custom-call | tf_op jit(solution)/shard_map/assemble/pallas_call | solution.py:410
  127.3 3.4 %copy.12 = f32[4,2,240,320]{2,3,1,0:T(8,128)} copy(f32[4,2,240,320]{3,2,1,0:T(8,128)} %assemble.1) | data formatting | bytes 4915200 | tf_op jit(solution)/shard_map/assemble/pallas_call | solution.py:410
